TPU v7x, 128 devices: a whole 4x4x4 slice. The times are simulated.
128 devices in a mesh: kv: 8 (over x, z_hi), seq: 16 (over y, z_lo, core).
Axes of the slice: x: 4, y: 4, z: 4 (z_hi: 2, z_lo: 2; z = z_hi * 2 + z_lo), core: 2. Of those that a mesh axis runs over, the one named last changes fastest.
Arguments:
- queries: bfloat16 [4096, 16384], P('seq', 'kv'), may hold values from -24 to 24
- keys: bfloat16 [4096, 1024], P('seq', 'kv'), may hold values from -24 to 24
- values: bfloat16 [4096, 1024], P('seq', 'kv'), may hold values from -6 to 6
- query_map: float32 [128, 128, 64], P('kv'), may hold values from -4 to 4
- key_map: float32 [128, 128, 64], P('kv'), may hold values from -4 to 4
Outputs:
- grad_query_map: float32 [128, 128, 64], P(('kv', 'seq'))
- grad_key_map: float32 [128, 128, 64], P(('kv', 'seq'))
All inputs are finite; a program needn't handle non-finite values.
Results may differ from a plain program's by a relative error of at most 0.00165.
Values may be sent and summed in bfloat16 or wider, within the bound.
No kernel may reach another device: no remote copies, remote signals or barrier semaphores. Data moves between devices by JAX's collectives and lax.ppermute only.
A program may use at most 128 MiB of HBM per device.

v0:
```python
import functools

import jax
import jax.numpy as jnp
from jax import lax
from jax.experimental import pallas as pl
from jax.experimental.pallas import tpu as pltpu
from jax.sharding import PartitionSpec as P

f32, bf16 = jnp.float32, jnp.bfloat16
HD = 128
FEAT = 64
CHUNK = 256
TOGETHER = 8
NT = (((1,), (1,)), ((), ()))
NN = (((1,), (0,)), ((), ()))
TN = (((0,), (0,)), ((), ()))


def dot(a, b, dims=NN):
    return lax.dot_general(a, b, dims, preferred_element_type=f32)


def lanes(*xs):
    return jnp.concatenate(xs, axis=1)


def rows(*xs):
    return jnp.concatenate(xs, axis=0)


def split(x):
    high = x.astype(bf16)
    return high, (x - high.astype(f32)).astype(bf16)


def first_half(shape):
    return lax.broadcasted_iota(jnp.int32, shape, 1) < FEAT


def half_sums(x):
    lo = first_half(x.shape)
    a = jnp.sum(jnp.where(lo, x, 0.0), axis=1, keepdims=True)
    b = jnp.sum(jnp.where(lo, 0.0, x), axis=1, keepdims=True)
    return a, b


def phi(logits):
    lo = first_half(logits.shape)
    a = jnp.max(jnp.where(lo, logits, -jnp.inf), axis=1, keepdims=True)
    b = jnp.max(jnp.where(lo, -jnp.inf, logits), axis=1, keepdims=True)
    e = jnp.exp(logits - jnp.where(lo, a, b))
    a, b = half_sums(e)
    return e * jnp.where(lo, 1.0 / a, 1.0 / b)


def phi_back(p, d):
    x = p * d
    a, b = half_sums(x)
    return x - p * jnp.where(first_half(x.shape), a, b)


def signed_pair(w):
    return rows(*split(lanes(w, -w)))


def lane_max(s):
    m = s[:, :128]
    for at in range(128, s.shape[1], 128):
        m = jnp.maximum(m, s[:, at : at + 128])
    return m


def teacher_kernel(x_ref, o_ref, score, *, block):
    total = x_ref.shape[0]
    exponent = 1.4426950408889634 / HD**0.5

    def scores(i):
        q = x_ref[i * block : (i + 1) * block, :HD]
        peak = None
        for j in range(i + 1):
            s = dot(q, x_ref[j * block : (j + 1) * block, HD : 2 * HD], NT)
            if j == i:
                r = lax.broadcasted_iota(jnp.int32, s.shape, 0)
                c = lax.broadcasted_iota(jnp.int32, s.shape, 1)
                s = jnp.where(r >= c, s, -1e30)
            score[i % 2, :, j * block : (j + 1) * block] = s
            m = lane_max(s)
            peak = m if peak is None else jnp.maximum(peak, m)
        return jnp.max(peak, axis=1, keepdims=True)

    def mix(i, peak):
        n = (i + 1) * block
        ve = lanes(x_ref[:n, 2 * HD :], jnp.ones((n, 128), bf16))
        shift = peak * exponent
        p = [
            jnp.exp2(score[i % 2, :, j * block : (j + 1) * block] * exponent - shift)
            for j in range(i + 1)
        ]
        if i == 0:
            high, low = split(p[0])
            acc = dot(lanes(high, low), rows(ve, ve))
        else:
            acc = dot(lanes(*(x.astype(bf16) for x in p)), ve)
        o_ref[i * block : (i + 1) * block, :] = (acc[:, :HD] / acc[:, HD:]).astype(bf16)

    peak = scores(0)
    for i in range(total // block):
        following = scores(i + 1) if (i + 1) * block < total else None
        mix(i, peak)
        peak = following


def teacher(x):
    total = x.shape[0]
    return pl.pallas_call(
        functools.partial(teacher_kernel, block=CHUNK),
        out_shape=jax.ShapeDtypeStruct((total, HD), bf16),
        scratch_shapes=[pltpu.VMEM((2, CHUNK, total), f32)],
        compiler_params=pltpu.CompilerParams(vmem_limit_bytes=56 << 20),
        name="teacher",
    )(x)


def student_kernel(x_ref, o_ref, wq_ref, wk_ref, gq_ref, gk_ref, fq_s, fk_s, st_s):
    total = x_ref.shape[0]
    count = total // CHUNK
    sl = [slice(c * CHUNK, (c + 1) * CHUNK) for c in range(count)]
    wq, wk = signed_pair(wq_ref[...]), signed_pair(wk_ref[...])
    one = jnp.ones((CHUNK, 128), bf16)

    def values_and_ones(c):
        return lanes(x_ref[sl[c], 2 * HD :], one)

    state = jnp.zeros((2 * FEAT, 256), f32)
    for g in range(0, count, TOGETHER):
        cs = range(g, min(g + TOGETHER, count))
        lq = [dot(lanes(x_ref[sl[c], :HD], x_ref[sl[c], :HD]), wq) for c in cs]
        lk = [dot(lanes(*[x_ref[sl[c], HD : 2 * HD]] * 2), wk) for c in cs]
        fk = [phi(x) for x in lk]
        fq = [phi(x) for x in lq]
        add = [dot(f.astype(bf16), values_and_ones(c), TN) for f, c in zip(fk, cs)]
        for i, c in enumerate(cs):
            fq_s[sl[c], :] = fq[i]
            fk_s[sl[c], :] = fk[i]
            st_s[c] = state.astype(bf16)
            state = state + add[i]

    r = lax.broadcasted_iota(jnp.int32, (CHUNK, CHUNK), 0)
    k = lax.broadcasted_iota(jnp.int32, (CHUNK, CHUNK), 1)
    later = jnp.zeros((2 * FEAT, 256), f32)
    gq = jnp.zeros((HD, 256), f32)
    gk = jnp.zeros((HD, 256), f32)
    for g in reversed(range(0, count, TOGETHER)):
        cs = list(reversed(range(g, min(g + TOGETHER, count))))
        every = range(len(cs))
        ve = [values_and_ones(c) for c in cs]
        st = [st_s[c] for c in cs]
        fq = [split(fq_s[sl[c], :]) for c in cs]
        fk = [split(fk_s[sl[c], :]) for c in cs]
        at = []
        for i in every:
            a = dot(fq[i][0], fk[i][0], NT)
            if cs[i] == 0:
                a = a + dot(lanes(*fq[i]), lanes(fk[i][1], fk[i][0]), NT)
            at.append(split(jnp.where(r >= k, a, 0.0)))
        nd = [dot(lanes(*at[i], fq[i][0]), rows(ve[i], ve[i], st[i])) for i in every]
        inv = [1.0 / x[:, HD:] for x in nd]
        out = [x[:, :HD] * y for x, y in zip(nd, inv)]
        dn = [(out[i] - o_ref[sl[cs[i]], :].astype(f32)) * inv[i] * (2.0 / total) for i in every]
        dd = [split(jnp.sum(dn[i] * out[i], axis=1, keepdims=True) * (-1.0 / 64)) for i in every]
        dd = [jnp.where(first_half((CHUNK, 128)), h.astype(f32), l.astype(f32)).astype(bf16) for h, l in dd]
        dx = [lanes(dn[i].astype(bf16), dd[i]) for i in every]
        da, dat = [], []
        for i in every:
            a, b = dot(dx[i], ve[i], NT), dot(ve[i], dx[i], NT)
            if cs[i] == 0:
                low = split(dn[i])[1]
                a, b = a + dot(low, ve[i][:, :HD], NT), b + dot(ve[i][:, :HD], low, NT)
            da.append(split(jnp.where(r >= k, a, 0.0)))
            dat.append(split(jnp.where(r <= k, b, 0.0)))
        after = []
        for i in every:
            after.append(later.astype(bf16))
            later = later + dot(fq[i][0], dx[i], TN)
        x = [dot(da[i][0], lanes(*fk[i])) for i in every]
        dfq = [x[i][:, :128] + x[i][:, 128:] + dot(da[i][1], fk[i][0]) + dot(dx[i], st[i], NT) for i in every]
        x = [dot(dat[i][0], lanes(*fq[i])) for i in every]
        dfk = [x[i][:, :128] + x[i][:, 128:] + dot(dat[i][1], fq[i][0]) + dot(ve[i], after[i], NT) for i in every]
        yq = [lanes(*split(phi_back(fq_s[sl[cs[i]], :], dfq[i]))) for i in every]
        yk = [lanes(*split(phi_back(fk_s[sl[cs[i]], :], dfk[i]))) for i in every]
        lo, hi = sl[cs[-1]].start, sl[cs[0]].stop
        gq = gq + dot(x_ref[lo:hi, :HD], rows(*yq[::-1]), TN)
        gk = gk + dot(x_ref[lo:hi, HD : 2 * HD], rows(*yk[::-1]), TN)

    def fold(g):
        g = g[:, :128] + g[:, 128:]
        return g[:, :FEAT] - g[:, FEAT:]

    gq_ref[...] = fold(gq)
    gk_ref[...] = fold(gk)


def student(x, o, wq, wk):
    total = x.shape[0]
    return pl.pallas_call(
        student_kernel,
        out_shape=[jax.ShapeDtypeStruct(wq.shape, f32)] * 2,
        scratch_shapes=[
            pltpu.VMEM((total, 2 * FEAT), f32),
            pltpu.VMEM((total, 2 * FEAT), f32),
            pltpu.VMEM((total // CHUNK, 2 * FEAT, 256), bf16),
        ],
        compiler_params=pltpu.CompilerParams(vmem_limit_bytes=56 << 20),
        name="student",
    )(x, o, wq, wk)


def shards(queries, keys, values, query_map, key_map):
    tok = queries.shape[0]
    peers = lax.axis_size("seq")
    mine = lax.axis_index("seq")
    kv = jnp.broadcast_to(lanes(keys, values)[None], (peers, tok, 2 * HD))
    qs = queries.reshape(tok, peers, HD).transpose(1, 0, 2)
    x = lax.all_to_all(jnp.concatenate([qs, kv], axis=2), "seq", 0, 0, tiled=True)
    x = x.reshape(peers * tok, 3 * HD)
    wq = lax.dynamic_index_in_dim(query_map, mine, 0, keepdims=False)
    wk = lax.dynamic_index_in_dim(key_map, mine, 0, keepdims=False)
    gq, gk = student(x, teacher(x), wq, wk)
    return gq[None], gk[None]


def solution(mesh):
    return jax.shard_map(
        shards,
        mesh=mesh,
        in_specs=(
            P("seq", "kv"),
            P("seq", "kv"),
            P("seq", "kv"),
            P("kv", None, None),
            P("kv", None, None),
        ),
        out_specs=(P(("kv", "seq"), None, None), P(("kv", "seq"), None, None)),
        check_vma=False,
    )
```

profile of v0, /device:TPU:99, one launch (start us, length us, event | category | flops | bytes accessed | tf_op | source)
XLA Modules:
  0.0 88.7 jit_solution(3962263826976800843)
XLA Ops:
  0.6 0.0 copy-start
  0.6 1.2 %copy-done = bf16[256,2048]{1,0:T(8,128)(2,1)S(1)} copy-done((bf16[256,2048]{1,0:T(8,128)(2,1)S(1)}, bf16[256,2048]{1,0:T(8,128)(2,1)}, u32[]{:S(2)}) %copy-start) | copy-done | bytes 1048600
  1.9 0.3 bitcast_bitcast_fusion
  2.1 0.9 %pad_maximum_fusion.1 = bf16[256,256]{1,0:T(8,128)(2,1)S(1)} fusion(bf16[256,128]{1,0:T(8,128)(2,1)} %param.7, bf16[256,128]{1,0:T(8,128)(2,1)} %param.6), kind=kLoop, calls=%fused_computation.2 | loop fusion | flops 262144 | bytes 262144 | tf_op jit(solution)/shard_map/concatenate | solution.py:25
  3.0 0.2 broadcast_in_dim.12
  3.2 2.1 %pad_maximum_fusion = bf16[16,256,384]{2,1,0:T(8,128)(2,1)} fusion(bf16[16,256,256]{2,1,0:T(8,128)(2,1)S(1)} %broadcast_in_dim.12, bf16[16,256,128]{2,1,0:T(8,128)(2,1)S(1)} %bitcast_bitcast_fusion), kind=kLoop, calls=%fused_computation | loop fusion | flops 6291456 | bytes 6291456 | tf_op jit(solution)/shard_map/concatenate | solution.py:225
  5.4 6.3 %all-to-all-start = ((bf16[16,256,384]{2,1,0:T(8,128)(2,1)}), bf16[16,256,384]{2,1,0:T(8,128)(2,1)}, u32[]{:S(2)}, u32[]{:S(2)}) async-start(bf16[16,256,384]{2,1,0:T(8,128)(2,1)} %pad_maximum_fusion), calls=%async_computation | async-start | bytes 6291456 | tf_op jit(solution)/shard_map/all_to_all | solution.py:225
  11.6 0.8 constant_dynamic-slice_fusion
  12.4 0.7 copy.8
  13.1 0.7 copy.9
  13.9 40.9 %all-to-all-done = bf16[16,256,384]{2,1,0:T(8,128)(2,1)} async-done(((bf16[16,256,384]{2,1,0:T(8,128)(2,1)}), bf16[16,256,384]{2,1,0:T(8,128)(2,1)}, u32[]{:S(2)}, u32[]{:S(2)}) %all-to-all-start) | async-done | bytes 3145760 | tf_op jit(solution)/shard_map/all_to_all | solution.py:225
  54.7 14.0 %teacher.1.o_ref = bf16[4096,128]{1,0:T(8,128)(2,1)} custom-call(bf16[4096,384]{1,0:T(8,128)(2,1)} %bitcast.1.x_ref), custom_call_target="tpu_custom_call" | custom-call | tf_op jit(solution)/shard_map/teacher/pallas_call | solution.py:116
  68.8 16.8 %student.1 = (f32[128,64]{1,0:T(8,128)}, f32[128,64]{1,0:T(8,128)}) custom-call(bf16[4096,384]{1,0:T(8,128)(2,1)} %bitcast.1.x_ref, bf16[4096,128]{1,0:T(8,128)(2,1)} %teacher.1.o_ref, f32[128,64]{1,0:T(8,128)} %bitcast.12, f32[128,64]{1,0:T(8,128)} %bitcast.13), custom_call_target="tpu_custom_call" | custom-call | tf_op jit(solution)/shard_map/student/pallas_call | solution.py:206
  85.6 1.5 %copy.10 = f32[1,128,64]{1,2,0:T(8,128)} copy(f32[1,128,64]{2,1,0:T(8,128)} %bitcast.15) | data formatting | bytes 65536
  87.2 1.5 %copy.11 = f32[1,128,64]{1,2,0:T(8,128)} copy(f32[1,128,64]{2,1,0:T(8,128)} %bitcast.14) | data formatting | bytes 65536
Async XLA Ops:
  0.6 1.2 %copy-start = (bf16[256,2048]{1,0:T(8,128)(2,1)S(1)}, bf16[256,2048]{1,0:T(8,128)(2,1)}, u32[]{:S(2)}) copy-start(bf16[256,2048]{1,0:T(8,128)(2,1)} %param.5) | copy-start | bytes 3145732
  5.4 49.4 %all-to-all-start = ((bf16[16,256,384]{2,1,0:T(8,128)(2,1)}), bf16[16,256,384]{2,1,0:T(8,128)(2,1)}, u32[]{:S(2)}, u32[]{:S(2)}) async-start(bf16[16,256,384]{2,1,0:T(8,128)(2,1)} %pad_maximum_fusion), calls=%async_computation | async-start | bytes 6291456 | tf_op jit(solution)/shard_map/all_to_all | solution.py:225
where the time goes:
time: 89.1 us; the launch traced here: 88.7 us
  waiting for transfers between devices  40.9 us (46%)
  Pallas kernels  30.9 us (35%)
  local copies, waits for them, and re-layouts  6.99 us (8%)
  starting transfers between devices  6.26 us (7%)
  other arithmetic  3.03 us (3%)
    all_to_all x1, waiting for transfers between devices, shards(): lax.all_to_all(jnp.concatenate([qs, kv], axis=2), 'seq', 0, 0, tiled=True)  40.9 us
    pallas_call x1, Pallas kernels, student(): pl.pallas_call(student_kernel, out_shape=[jax.ShapeDtypeStruct(wq.shape,...  16.8 us
    pallas_call x1, Pallas kernels, teacher(): pl.pallas_call(functools.partial(teacher_kernel, block=CHUNK), out_shape=...  14 us
    all_to_all x1, starting transfers between devices, shards(): lax.all_to_all(jnp.concatenate([qs, kv], axis=2), 'seq', 0, 0, tiled=True)  6.26 us
    unnamed x4, local copies, waits for them, and re-layouts  4.29 us
    concatenate x1, other arithmetic, shards(): jnp.concatenate([qs, kv], axis=2)  2.14 us
  transfers between devices with their start and end apart: 1, of which 1 were waited for; matrix products, arithmetic and copies ran while one was open for 3% of the time, Pallas kernels for 0%

commit v1 on v0

--- a/solution.py
+++ b/solution.py
@@ -60,10 +60,6 @@
     return x - p * jnp.where(first_half(x.shape), a, b)
 
 
-def signed_pair(w):
-    return rows(*split(lanes(w, -w)))
-
-
 def lane_max(s):
     m = s[:, :128]
     for at in range(128, s.shape[1], 128):
@@ -71,15 +67,15 @@
     return m
 
 
-def teacher_kernel(x_ref, o_ref, score, *, block):
-    total = x_ref.shape[0]
+def teach(q_ref, kv_ref, o_ref, score, block):
+    total = q_ref.shape[0]
     exponent = 1.4426950408889634 / HD**0.5
 
     def scores(i):
-        q = x_ref[i * block : (i + 1) * block, :HD]
+        q = q_ref[i * block : (i + 1) * block, :]
         peak = None
         for j in range(i + 1):
-            s = dot(q, x_ref[j * block : (j + 1) * block, HD : 2 * HD], NT)
+            s = dot(q, kv_ref[j * block : (j + 1) * block, :HD], NT)
             if j == i:
                 r = lax.broadcasted_iota(jnp.int32, s.shape, 0)
                 c = lax.broadcasted_iota(jnp.int32, s.shape, 1)
@@ -91,7 +87,7 @@
 
     def mix(i, peak):
         n = (i + 1) * block
-        ve = lanes(x_ref[:n, 2 * HD :], jnp.ones((n, 128), bf16))
+        ve = lanes(kv_ref[:n, HD:], jnp.ones((n, 128), bf16))
         shift = peak * exponent
         p = [
             jnp.exp2(score[i % 2, :, j * block : (j + 1) * block] * exponent - shift)
@@ -111,40 +107,26 @@
         peak = following
 
 
-def teacher(x):
-    total = x.shape[0]
-    return pl.pallas_call(
-        functools.partial(teacher_kernel, block=CHUNK),
-        out_shape=jax.ShapeDtypeStruct((total, HD), bf16),
-        scratch_shapes=[pltpu.VMEM((2, CHUNK, total), f32)],
-        compiler_params=pltpu.CompilerParams(vmem_limit_bytes=56 << 20),
-        name="teacher",
-    )(x)
-
-
-def student_kernel(x_ref, o_ref, wq_ref, wk_ref, gq_ref, gk_ref, fq_s, fk_s, st_s):
-    total = x_ref.shape[0]
+def signed_pair(w):
+    return lanes(*split(rows(w, -w)))
+
+
+def whole(a):
+    return pl.BlockSpec(a.shape, lambda i, m: (0,) * len(a.shape))
+
+
+def head_block(w):
+    return pl.BlockSpec((1,) + w.shape[1:], lambda i, m: (m[0], 0, 0))
+
+
+def learn(q_ref, kv_ref, o_ref, fq_s, fk_s, st_s, gq_ref, gk_ref):
+    total = q_ref.shape[0]
     count = total // CHUNK
     sl = [slice(c * CHUNK, (c + 1) * CHUNK) for c in range(count)]
-    wq, wk = signed_pair(wq_ref[...]), signed_pair(wk_ref[...])
     one = jnp.ones((CHUNK, 128), bf16)
 
     def values_and_ones(c):
-        return lanes(x_ref[sl[c], 2 * HD :], one)
-
-    state = jnp.zeros((2 * FEAT, 256), f32)
-    for g in range(0, count, TOGETHER):
-        cs = range(g, min(g + TOGETHER, count))
-        lq = [dot(lanes(x_ref[sl[c], :HD], x_ref[sl[c], :HD]), wq) for c in cs]
-        lk = [dot(lanes(*[x_ref[sl[c], HD : 2 * HD]] * 2), wk) for c in cs]
-        fk = [phi(x) for x in lk]
-        fq = [phi(x) for x in lq]
-        add = [dot(f.astype(bf16), values_and_ones(c), TN) for f, c in zip(fk, cs)]
-        for i, c in enumerate(cs):
-            fq_s[sl[c], :] = fq[i]
-            fk_s[sl[c], :] = fk[i]
-            st_s[c] = state.astype(bf16)
-            state = state + add[i]
+        return lanes(kv_ref[sl[c], HD:], one)
 
     r = lax.broadcasted_iota(jnp.int32, (CHUNK, CHUNK), 0)
     k = lax.broadcasted_iota(jnp.int32, (CHUNK, CHUNK), 1)
@@ -190,44 +172,108 @@
         yq = [lanes(*split(phi_back(fq_s[sl[cs[i]], :], dfq[i]))) for i in every]
         yk = [lanes(*split(phi_back(fk_s[sl[cs[i]], :], dfk[i]))) for i in every]
         lo, hi = sl[cs[-1]].start, sl[cs[0]].stop
-        gq = gq + dot(x_ref[lo:hi, :HD], rows(*yq[::-1]), TN)
-        gk = gk + dot(x_ref[lo:hi, HD : 2 * HD], rows(*yk[::-1]), TN)
+        gq = gq + dot(q_ref[lo:hi, :], rows(*yq[::-1]), TN)
+        gk = gk + dot(kv_ref[lo:hi, :HD], rows(*yk[::-1]), TN)
 
     def fold(g):
         g = g[:, :128] + g[:, 128:]
-        return g[:, :FEAT] - g[:, FEAT:]
+        return g.T[:FEAT] - g.T[FEAT:]
 
     gq_ref[...] = fold(gq)
     gk_ref[...] = fold(gk)
 
 
-def student(x, o, wq, wk):
-    total = x.shape[0]
+def features(q_ref, kv_ref, wq, wk, fq_s, fk_s, st_s):
+    one = jnp.ones((CHUNK, 128), bf16)
+    state = jnp.zeros((2 * FEAT, 256), f32)
+    count = q_ref.shape[0] // CHUNK
+    sl = [slice(c * CHUNK, (c + 1) * CHUNK) for c in range(count)]
+    for g in range(0, count, TOGETHER):
+        cs = range(g, min(g + TOGETHER, count))
+        lq = [dot(lanes(*[q_ref[sl[c], :]] * 2), wq, NT) for c in cs]
+        lk = [dot(lanes(*[kv_ref[sl[c], :HD]] * 2), wk, NT) for c in cs]
+        fk = [phi(x) for x in lk]
+        fq = [phi(x) for x in lq]
+        add = [dot(f.astype(bf16), lanes(kv_ref[sl[c], HD:], one), TN) for f, c in zip(fk, cs)]
+        for i, c in enumerate(cs):
+            fq_s[sl[c], :] = fq[i]
+            fk_s[sl[c], :] = fk[i]
+            st_s[c] = state.astype(bf16)
+            state = state + add[i]
+
+
+def assemble(mine, pieces, kv_ref):
+    tok = pieces[0].shape[1]
+    y, core = mine // 4, mine % 2
+    spans = len(pieces) // 2
+    for side in range(2):
+        c = core if side == 0 else 1 - core
+        for d in range(spans):
+            from_y = (y + spans - d) % spans
+            for z in range(2):
+                at = pl.multiple_of((from_y * 4 + z * 2 + c) * tok, tok)
+                kv_ref[pl.ds(at, tok), :] = pieces[side * spans + d][z]
+
+
+def layer_kernel(mine_ref, q_ref, *refs):
+    *pieces, wq_ref, wk_ref, gq_ref, gk_ref, kv_s, o_s, score, fq_s, fk_s, st_s = refs
+    assemble(mine_ref[0], pieces, kv_s)
+    features(q_ref, kv_s, signed_pair(wq_ref[0]), signed_pair(wk_ref[0]), fq_s, fk_s, st_s)
+    teach(q_ref, kv_s, o_s, score, CHUNK)
+    learn(q_ref, kv_s, o_s, fq_s, fk_s, st_s, gq_ref, gk_ref)
+
+
+def layer(mine, q, pieces, wq, wk):
+    total = q.shape[0]
+    out = [jax.ShapeDtypeStruct((FEAT, HD), f32)] * 2
     return pl.pallas_call(
-        student_kernel,
-        out_shape=[jax.ShapeDtypeStruct(wq.shape, f32)] * 2,
-        scratch_shapes=[
-            pltpu.VMEM((total, 2 * FEAT), f32),
-            pltpu.VMEM((total, 2 * FEAT), f32),
-            pltpu.VMEM((total // CHUNK, 2 * FEAT, 256), bf16),
-        ],
+        layer_kernel,
+        grid_spec=pltpu.PrefetchScalarGridSpec(
+            num_scalar_prefetch=1,
+            grid=(1,),
+            in_specs=[whole(q)] + [whole(a) for a in pieces] + [head_block(wq), head_block(wk)],
+            out_specs=[whole(o) for o in out],
+            scratch_shapes=[
+                pltpu.VMEM((total, 2 * HD), bf16),
+                pltpu.VMEM((total, HD), bf16),
+                pltpu.VMEM((2, CHUNK, total), f32),
+                pltpu.VMEM((total, 2 * FEAT), f32),
+                pltpu.VMEM((total, 2 * FEAT), f32),
+                pltpu.VMEM((total // CHUNK, 2 * FEAT, 256), bf16),
+            ],
+        ),
+        out_shape=out,
         compiler_params=pltpu.CompilerParams(vmem_limit_bytes=56 << 20),
-        name="student",
-    )(x, o, wq, wk)
+        name="layer",
+    )(mine, q, *pieces, wq, wk)
+
+
+def step(x, move):
+    return lax.ppermute(x, "seq", [(i, move(i)) for i in range(lax.axis_size("seq"))])
 
 
 def shards(queries, keys, values, query_map, key_map):
     tok = queries.shape[0]
     peers = lax.axis_size("seq")
     mine = lax.axis_index("seq")
-    kv = jnp.broadcast_to(lanes(keys, values)[None], (peers, tok, 2 * HD))
+    here = lanes(keys, values)
+    over = step(here, lambda i: i ^ 2)
+    low = mine // 2 % 2 == 0
+    pair = jnp.stack([jnp.where(low, here, over), jnp.where(low, over, here)])
+    up = lambda x: step(x, lambda i: (i + 4) % peers)
+    down = lambda x: step(x, lambda i: (i - 4) % peers)
+    pieces = [pair] + [step(pair, lambda i, d=d: (i + 4 * d) % peers) for d in range(1, peers // 4)]
+    pieces = pieces + [step(x, lambda i: i ^ 1) for x in pieces]
     qs = queries.reshape(tok, peers, HD).transpose(1, 0, 2)
-    x = lax.all_to_all(jnp.concatenate([qs, kv], axis=2), "seq", 0, 0, tiled=True)
-    x = x.reshape(peers * tok, 3 * HD)
-    wq = lax.dynamic_index_in_dim(query_map, mine, 0, keepdims=False)
-    wk = lax.dynamic_index_in_dim(key_map, mine, 0, keepdims=False)
-    gq, gk = student(x, teacher(x), wq, wk)
-    return gq[None], gk[None]
+    q = lax.all_to_all(qs, "seq", 0, 0, tiled=True).reshape(peers * tok, HD)
+    gq, gk = layer(
+        mine.astype(jnp.int32).reshape(1),
+        q,
+        pieces,
+        query_map.transpose(0, 2, 1),
+        key_map.transpose(0, 2, 1),
+    )
+    return gq.T[None], gk.T[None]
 
 
 def solution(mesh):

time: 89.1 us -> 67.8 us (0.76)
  the two profiles are of different devices: /device:TPU:99 before, /device:TPU:1 now
where the time goes in v1:
time: 67.8 us; the launch traced here: 67.5 us
  Pallas kernels  26.5 us (39%)
  waiting for transfers between devices  20 us (29%)
  starting transfers between devices  16.3 us (24%)
  local copies, waits for them, and re-layouts  3.91 us (6%)
  between operations  0.76 us (1%)
    pallas_call x1, Pallas kernels, layer(): pl.pallas_call(layer_kernel, grid_spec=pltpu.PrefetchScalarGridSpec(num_s...  26.5 us
    ppermute x8, waiting for transfers between devices, step(): lax.ppermute(x, 'seq', [(i, move(i)) for i in range(lax.axis_size('seq'))])  20 us
    ppermute x8, starting transfers between devices, step(): lax.ppermute(x, 'seq', [(i, move(i)) for i in range(lax.axis_size('seq'))])  10.9 us
    all_to_all x1, starting transfers between devices, shards(): q = lax.all_to_all(qs, 'seq', 0, 0, tiled=True).reshape(peers * tok, HD)  5.44 us
    unnamed x21, local copies, waits for them, and re-layouts  2.64 us
  transfers between devices with their start and end apart: 9, of which 3 were waited for; matrix products, arithmetic and copies ran while one was open for 2% of the time, Pallas kernels for 0%

profile of v1, /device:TPU:1, one launch (start us, length us, event | category | flops | bytes accessed | tf_op | source)
XLA Modules:
  0.0 67.5 jit_solution(902116711687620207)
XLA Ops:
  0.6 0.0 copy-start
  0.6 0.0 copy-start.9
  0.7 1.0 %constant_dynamic-update-slice_fusion.1 = bf16[256,256]{1,0:T(8,128)(2,1)S(1)} fusion(bf16[256,128]{1,0:T(8,128)(2,1)} %param.6), kind=kLoop, calls=%fused_computation.5 | loop fusion | bytes 131072
  1.6 0.0 copy-done.9
  1.6 2.5 %collective-permute-start = (bf16[256,256]{1,0:T(8,128)(2,1)S(1)}, bf16[256,256]{1,0:T(8,128)(2,1)S(1)}, u32[]{:S(2)}, u32[]{:S(2)}) collective-permute-start(bf16[256,256]{1,0:T(8,128)(2,1)S(1)} %constant_dynamic-update-slice_fusion), channel_id=1, source_target_pairs={{0,2},{1,3},{2,0},{3,1},{4,6},{5,7},{6,4},{7,5},{8,10},{9,11},{10,... | collective-permute-start | bytes 393224 | tf_op jit(solution)/shard_map/ppermute | solution.py:252
  4.2 0.0 copy-done
  4.2 1.3 %bitcast_bitcast_fusion = bf16[16,256,128]{2,1,0:T(8,128)(2,1)} fusion(bf16[256,2048]{1,0:T(8,128)(2,1)S(1)} %copy-done), kind=kLoop, calls=%fused_computation | loop fusion | bytes 2097152 | tf_op jit(solution)/shard_map/transpose | solution.py:267
  5.5 5.4 %all-to-all-start = ((bf16[16,256,128]{2,1,0:T(8,128)(2,1)}), bf16[16,256,128]{2,1,0:T(8,128)(2,1)S(1)}, u32[]{:S(2)}, u32[]{:S(2)}) async-start(bf16[16,256,128]{2,1,0:T(8,128)(2,1)} %bitcast_bitcast_fusion), calls=%async_computation | async-start | bytes 2097152 | tf_op jit(solution)/shard_map/all_to_all | solution.py:268
  10.9 0.0 collective-permute-done
  11.0 0.0 copy-start.2
  11.0 1.5 %collective-permute-start.1 = (bf16[2,256,256]{2,1,0:T(8,128)(2,1)S(1)}, bf16[2,256,256]{2,1,0:T(8,128)(2,1)S(1)}, u32[]{:S(2)}, u32[]{:S(2)}) collective-permute-start(bf16[2,256,256]{2,1,0:T(8,128)(2,1)S(1)} %pad_maximum_fusion.refs_0_), channel_id=1, source_target_pairs={{0,4},{1,5},{2,6},{3,7},{4,8},{5,9},{6,10},{7,11},{8,12},{9,13},{1... | collective-permute-start | bytes 786440 | tf_op jit(solution)/shard_map/ppermute | solution.py:252
  12.4 2.4 %collective-permute-start.2 = (bf16[2,256,256]{2,1,0:T(8,128)(2,1)S(1)}, bf16[2,256,256]{2,1,0:T(8,128)(2,1)S(1)}, u32[]{:S(2)}, u32[]{:S(2)}) collective-permute-start(bf16[2,256,256]{2,1,0:T(8,128)(2,1)S(1)} %pad_maximum_fusion.refs_0_), channel_id=1, source_target_pairs={{0,8},{1,9},{2,10},{3,11},{4,12},{5,13},{6,14},{7,15},{8,0},{9,1},... | collective-permute-start | bytes 786440 | tf_op jit(solution)/shard_map/ppermute | solution.py:252
  14.8 1.2 %collective-permute-start.3 = (bf16[2,256,256]{2,1,0:T(8,128)(2,1)S(1)}, bf16[2,256,256]{2,1,0:T(8,128)(2,1)S(1)}, u32[]{:S(2)}, u32[]{:S(2)}) collective-permute-start(bf16[2,256,256]{2,1,0:T(8,128)(2,1)S(1)} %pad_maximum_fusion.refs_0_), channel_id=1, source_target_pairs={{0,12},{1,13},{2,14},{3,15},{4,0},{5,1},{6,2},{7,3},{8,4},{9,5},{1... | collective-permute-start | bytes 786440 | tf_op jit(solution)/shard_map/ppermute | solution.py:252
  16.0 1.2 %collective-permute-start.4 = (bf16[2,256,256]{2,1,0:T(8,128)(2,1)S(1)}, bf16[2,256,256]{2,1,0:T(8,128)(2,1)S(1)}, u32[]{:S(2)}, u32[]{:S(2)}) collective-permute-start(bf16[2,256,256]{2,1,0:T(8,128)(2,1)S(1)} %pad_maximum_fusion.refs_0_), channel_id=1, source_target_pairs={{0,1},{1,0},{2,3},{3,2},{4,5},{5,4},{6,7},{7,6},{8,9},{9,8},{10,11... | collective-permute-start | bytes 786440 | tf_op jit(solution)/shard_map/ppermute | solution.py:252
  17.2 14.1 %collective-permute-done.1.refs_1_ = bf16[2,256,256]{2,1,0:T(8,128)(2,1)S(1)} collective-permute-done((bf16[2,256,256]{2,1,0:T(8,128)(2,1)S(1)}, bf16[2,256,256]{2,1,0:T(8,128)(2,1)S(1)}, u32[]{:S(2)}, u32[]{:S(2)}) %collective-permute-start.1) | collective-permute-done | bytes 262176 | tf_op jit(solution)/shard_map/ppermute | solution.py:252
  31.3 0.0 copy-start.3
  31.3 1.0 %collective-permute-start.5 = (bf16[2,256,256]{2,1,0:T(8,128)(2,1)S(1)}, bf16[2,256,256]{2,1,0:T(8,128)(2,1)S(1)}, u32[]{:S(2)}, u32[]{:S(2)}) collective-permute-start(bf16[2,256,256]{2,1,0:T(8,128)(2,1)S(1)} %collective-permute-done.1.refs_1_), channel_id=1, source_target_pairs={{0,1},{1,0},{2,3},{3,2},{4,5},{5,4},{6,7},{7,6},{8,9},{9,8},{10,11... | collective-permute-start | bytes 786440 | tf_op jit(solution)/shard_map/ppermute | solution.py:252
  32.3 5.0 %collective-permute-done.2.refs_2_ = bf16[2,256,256]{2,1,0:T(8,128)(2,1)S(1)} collective-permute-done((bf16[2,256,256]{2,1,0:T(8,128)(2,1)S(1)}, bf16[2,256,256]{2,1,0:T(8,128)(2,1)S(1)}, u32[]{:S(2)}, u32[]{:S(2)}) %collective-permute-start.2) | collective-permute-done | bytes 262176 | tf_op jit(solution)/shard_map/ppermute | solution.py:252
  37.3 0.0 copy-start.4
  37.3 0.9 %collective-permute-start.6 = (bf16[2,256,256]{2,1,0:T(8,128)(2,1)S(1)}, bf16[2,256,256]{2,1,0:T(8,128)(2,1)S(1)}, u32[]{:S(2)}, u32[]{:S(2)}) collective-permute-start(bf16[2,256,256]{2,1,0:T(8,128)(2,1)S(1)} %collective-permute-done.2.refs_2_), channel_id=1, source_target_pairs={{0,1},{1,0},{2,3},{3,2},{4,5},{5,4},{6,7},{7,6},{8,9},{9,8},{10,11... | collective-permute-start | bytes 786440 | tf_op jit(solution)/shard_map/ppermute | solution.py:252
  38.2 0.0 collective-permute-done.3.refs_3_
  38.2 0.0 copy-start.5
  38.2 0.3 collective-permute-start.7
  38.5 0.0 collective-permute-done.4.refs_4_
  38.5 0.0 copy-start.6
  38.5 0.0 collective-permute-done.5.refs_5_
  38.5 0.0 copy-start.7
  38.5 0.9 %collective-permute-done.6.refs_6_ = bf16[2,256,256]{2,1,0:T(8,128)(2,1)S(1)} collective-permute-done((bf16[2,256,256]{2,1,0:T(8,128)(2,1)S(1)}, bf16[2,256,256]{2,1,0:T(8,128)(2,1)S(1)}, u32[]{:S(2)}, u32[]{:S(2)}) %collective-permute-start.6) | collective-permute-done | bytes 262176 | tf_op jit(solution)/shard_map/ppermute | solution.py:252
  39.4 0.0 copy-done.7
  39.4 0.0 copy-start.8
  39.4 0.7 %copy-done.8 = bf16[2,256,256]{2,1,0:T(8,128)(2,1)} copy-done((bf16[2,256,256]{2,1,0:T(8,128)(2,1)}, bf16[2,256,256]{2,1,0:T(8,128)(2,1)S(1)}, u32[]{:S(2)}) %copy-start.8) | copy-done | bytes 262168
  40.1 0.0 collective-permute-done.7.refs_7_
  40.1 0.0 all-to-all-done
  40.1 0.0 copy-start.1
  40.1 0.0 copy-done.2
  40.1 0.0 copy-done.3
  40.1 0.0 copy-done.4
  40.1 0.0 copy-done.5
  40.1 0.0 copy-done.6
  40.1 0.9 %copy-done.1 = bf16[16,256,128]{2,1,0:T(8,128)(2,1)} copy-done((bf16[16,256,128]{2,1,0:T(8,128)(2,1)}, bf16[16,256,128]{2,1,0:T(8,128)(2,1)S(1)}, u32[]{:S(2)}) %copy-start.1) | copy-done | bytes 1048600
  41.1 26.5 %layer.1 = (f32[64,128]{1,0:T(8,128)}, f32[64,128]{1,0:T(8,128)}) custom-call(s32[1]{0:T(128)} %bitcast.mine_ref, bf16[4096,128]{1,0:T(8,128)(2,1)} %bitcast.21, bf16[2,256,256]{2,1,0:T(8,128)(2,1)} %copy-done.2, bf16[2,256,256]{2,1,0:T(8,128)(2,1)} %copy-done.3, bf16[2,256,256]{2,1,0:T(8,128)(2,1)} %copy-done.4, bf16[2,256,256]{2,1,0:T(8,128)(2,1)} %copy-done.5, ...), custom_call_target="tpu_custom_call" | custom-call | tf_op jit(solution)/shard_map/layer/pallas_call | solution.py:229
  (3 shorter events, 0.1 us)
Async XLA Ops:
  0.6 3.6 %copy-start = (bf16[256,2048]{1,0:T(8,128)(2,1)S(1)}, bf16[256,2048]{1,0:T(8,128)(2,1)}, u32[]{:S(2)}) copy-start(bf16[256,2048]{1,0:T(8,128)(2,1)} %param.5) | copy-start | bytes 3145732
  0.6 1.0 %copy-start.9 = (bf16[256,128]{1,0:T(8,128)(2,1)S(1)}, bf16[256,128]{1,0:T(8,128)(2,1)}, u32[]{:S(2)}) copy-start(bf16[256,128]{1,0:T(8,128)(2,1)} %param.7) | copy-start | bytes 196612
  1.6 9.2 %collective-permute-start = (bf16[256,256]{1,0:T(8,128)(2,1)S(1)}, bf16[256,256]{1,0:T(8,128)(2,1)S(1)}, u32[]{:S(2)}, u32[]{:S(2)}) collective-permute-start(bf16[256,256]{1,0:T(8,128)(2,1)S(1)} %constant_dynamic-update-slice_fusion), channel_id=1, source_target_pairs={{0,2},{1,3},{2,0},{3,1},{4,6},{5,7},{6,4},{7,5},{8,10},{9,11},{10,... | collective-permute-start | bytes 393224 | tf_op jit(solution)/shard_map/ppermute | solution.py:252
  5.5 34.6 %all-to-all-start = ((bf16[16,256,128]{2,1,0:T(8,128)(2,1)}), bf16[16,256,128]{2,1,0:T(8,128)(2,1)S(1)}, u32[]{:S(2)}, u32[]{:S(2)}) async-start(bf16[16,256,128]{2,1,0:T(8,128)(2,1)} %bitcast_bitcast_fusion), calls=%async_computation | async-start | bytes 2097152 | tf_op jit(solution)/shard_map/all_to_all | solution.py:268
  11.0 29.1 %copy-start.2 = (bf16[2,256,256]{2,1,0:T(8,128)(2,1)}, bf16[2,256,256]{2,1,0:T(8,128)(2,1)S(1)}, u32[]{:S(2)}) copy-start(bf16[2,256,256]{2,1,0:T(8,128)(2,1)S(1)} %pad_maximum_fusion.refs_0_) | copy-start | bytes 786436
  11.0 20.3 %collective-permute-start.1 = (bf16[2,256,256]{2,1,0:T(8,128)(2,1)S(1)}, bf16[2,256,256]{2,1,0:T(8,128)(2,1)S(1)}, u32[]{:S(2)}, u32[]{:S(2)}) collective-permute-start(bf16[2,256,256]{2,1,0:T(8,128)(2,1)S(1)} %pad_maximum_fusion.refs_0_), channel_id=1, source_target_pairs={{0,4},{1,5},{2,6},{3,7},{4,8},{5,9},{6,10},{7,11},{8,12},{9,13},{1... | collective-permute-start | bytes 786440 | tf_op jit(solution)/shard_map/ppermute | solution.py:252
  12.4 24.9 %collective-permute-start.2 = (bf16[2,256,256]{2,1,0:T(8,128)(2,1)S(1)}, bf16[2,256,256]{2,1,0:T(8,128)(2,1)S(1)}, u32[]{:S(2)}, u32[]{:S(2)}) collective-permute-start(bf16[2,256,256]{2,1,0:T(8,128)(2,1)S(1)} %pad_maximum_fusion.refs_0_), channel_id=1, source_target_pairs={{0,8},{1,9},{2,10},{3,11},{4,12},{5,13},{6,14},{7,15},{8,0},{9,1},... | collective-permute-start | bytes 786440 | tf_op jit(solution)/shard_map/ppermute | solution.py:252
  14.8 23.4 %collective-permute-start.3 = (bf16[2,256,256]{2,1,0:T(8,128)(2,1)S(1)}, bf16[2,256,256]{2,1,0:T(8,128)(2,1)S(1)}, u32[]{:S(2)}, u32[]{:S(2)}) collective-permute-start(bf16[2,256,256]{2,1,0:T(8,128)(2,1)S(1)} %pad_maximum_fusion.refs_0_), channel_id=1, source_target_pairs={{0,12},{1,13},{2,14},{3,15},{4,0},{5,1},{6,2},{7,3},{8,4},{9,5},{1... | collective-permute-start | bytes 786440 | tf_op jit(solution)/shard_map/ppermute | solution.py:252
  16.0 22.5 %collective-permute-start.4 = (bf16[2,256,256]{2,1,0:T(8,128)(2,1)S(1)}, bf16[2,256,256]{2,1,0:T(8,128)(2,1)S(1)}, u32[]{:S(2)}, u32[]{:S(2)}) collective-permute-start(bf16[2,256,256]{2,1,0:T(8,128)(2,1)S(1)} %pad_maximum_fusion.refs_0_), channel_id=1, source_target_pairs={{0,1},{1,0},{2,3},{3,2},{4,5},{5,4},{6,7},{7,6},{8,9},{9,8},{10,11... | collective-permute-start | bytes 786440 | tf_op jit(solution)/shard_map/ppermute | solution.py:252
  31.3 8.8 %copy-start.3 = (bf16[2,256,256]{2,1,0:T(8,128)(2,1)}, bf16[2,256,256]{2,1,0:T(8,128)(2,1)S(1)}, u32[]{:S(2)}) copy-start(bf16[2,256,256]{2,1,0:T(8,128)(2,1)S(1)} %collective-permute-done.1.refs_1_) | copy-start | bytes 786436
  31.3 7.2 %collective-permute-start.5 = (bf16[2,256,256]{2,1,0:T(8,128)(2,1)S(1)}, bf16[2,256,256]{2,1,0:T(8,128)(2,1)S(1)}, u32[]{:S(2)}, u32[]{:S(2)}) collective-permute-start(bf16[2,256,256]{2,1,0:T(8,128)(2,1)S(1)} %collective-permute-done.1.refs_1_), channel_id=1, source_target_pairs={{0,1},{1,0},{2,3},{3,2},{4,5},{5,4},{6,7},{7,6},{8,9},{9,8},{10,11... | collective-permute-start | bytes 786440 | tf_op jit(solution)/shard_map/ppermute | solution.py:252
  37.3 2.8 %copy-start.4 = (bf16[2,256,256]{2,1,0:T(8,128)(2,1)}, bf16[2,256,256]{2,1,0:T(8,128)(2,1)S(1)}, u32[]{:S(2)}) copy-start(bf16[2,256,256]{2,1,0:T(8,128)(2,1)S(1)} %collective-permute-done.2.refs_2_) | copy-start | bytes 786436
  37.3 2.0 %collective-permute-start.6 = (bf16[2,256,256]{2,1,0:T(8,128)(2,1)S(1)}, bf16[2,256,256]{2,1,0:T(8,128)(2,1)S(1)}, u32[]{:S(2)}, u32[]{:S(2)}) collective-permute-start(bf16[2,256,256]{2,1,0:T(8,128)(2,1)S(1)} %collective-permute-done.2.refs_2_), channel_id=1, source_target_pairs={{0,1},{1,0},{2,3},{3,2},{4,5},{5,4},{6,7},{7,6},{8,9},{9,8},{10,11... | collective-permute-start | bytes 786440 | tf_op jit(solution)/shard_map/ppermute | solution.py:252
  38.2 1.9 %copy-start.5 = (bf16[2,256,256]{2,1,0:T(8,128)(2,1)}, bf16[2,256,256]{2,1,0:T(8,128)(2,1)S(1)}, u32[]{:S(2)}) copy-start(bf16[2,256,256]{2,1,0:T(8,128)(2,1)S(1)} %collective-permute-done.3.refs_3_) | copy-start | bytes 786436
  38.2 1.9 %collective-permute-start.7 = (bf16[2,256,256]{2,1,0:T(8,128)(2,1)S(1)}, bf16[2,256,256]{2,1,0:T(8,128)(2,1)}, u32[]{:S(2)}, u32[]{:S(2)}) collective-permute-start(bf16[2,256,256]{2,1,0:T(8,128)(2,1)S(1)} %collective-permute-done.3.refs_3_), channel_id=1, source_target_pairs={{0,1},{1,0},{2,3},{3,2},{4,5},{5,4},{6,7},{7,6},{8,9},{9,8},{10,11... | collective-permute-start | bytes 786440 | tf_op jit(solution)/shard_map/ppermute | solution.py:252
  38.5 1.6 %copy-start.6 = (bf16[2,256,256]{2,1,0:T(8,128)(2,1)}, bf16[2,256,256]{2,1,0:T(8,128)(2,1)S(1)}, u32[]{:S(2)}) copy-start(bf16[2,256,256]{2,1,0:T(8,128)(2,1)S(1)} %collective-permute-done.4.refs_4_) | copy-start | bytes 786436
  38.5 0.9 %copy-start.7 = (bf16[2,256,256]{2,1,0:T(8,128)(2,1)}, bf16[2,256,256]{2,1,0:T(8,128)(2,1)S(1)}, u32[]{:S(2)}) copy-start(bf16[2,256,256]{2,1,0:T(8,128)(2,1)S(1)} %collective-permute-done.5.refs_5_) | copy-start | bytes 786436
  39.4 0.7 %copy-start.8 = (bf16[2,256,256]{2,1,0:T(8,128)(2,1)}, bf16[2,256,256]{2,1,0:T(8,128)(2,1)S(1)}, u32[]{:S(2)}) copy-start(bf16[2,256,256]{2,1,0:T(8,128)(2,1)S(1)} %collective-permute-done.6.refs_6_) | copy-start | bytes 786436
  40.1 1.0 %copy-start.1 = (bf16[16,256,128]{2,1,0:T(8,128)(2,1)}, bf16[16,256,128]{2,1,0:T(8,128)(2,1)S(1)}, u32[]{:S(2)}) copy-start(bf16[16,256,128]{2,1,0:T(8,128)(2,1)S(1)} %all-to-all-done) | copy-start | bytes 3145732

commit v2 on v1

--- a/solution.py
+++ b/solution.py
@@ -183,47 +183,77 @@
     gk_ref[...] = fold(gk)
 
 
-def features(q_ref, kv_ref, wq, wk, fq_s, fk_s, st_s):
+def query_features_kernel(mine_ref, q_ref, w_ref, f_ref):
+    w = signed_pair(w_ref[0])
+    sl = [slice(at, at + CHUNK) for at in range(0, q_ref.shape[0], CHUNK)]
+    for g in range(0, len(sl), TOGETHER):
+        group = sl[g : g + TOGETHER]
+        logits = [dot(lanes(*[q_ref[x, :]] * 2), w, NT) for x in group]
+        fq = [phi(x) for x in logits]
+        for x, f in zip(group, fq):
+            f_ref[x, :] = f
+
+
+IN_VMEM = pl.BlockSpec(memory_space=pltpu.VMEM)
+
+
+def in_vmem(x):
+    return pltpu.with_memory_space_constraint(x, pltpu.VMEM)
+
+
+def query_features(mine, q, w):
+    return pl.pallas_call(
+        query_features_kernel,
+        grid_spec=pltpu.PrefetchScalarGridSpec(
+            num_scalar_prefetch=1,
+            grid=(1,),
+            in_specs=[IN_VMEM, head_block(w)],
+            out_specs=IN_VMEM,
+        ),
+        out_shape=jax.ShapeDtypeStruct((q.shape[0], 2 * FEAT), f32),
+        compiler_params=pltpu.CompilerParams(vmem_limit_bytes=48 << 20),
+        name="query_features",
+    )(mine, in_vmem(q), w)
+
+
+def key_features(kv_ref, wk, fk_s, st_s):
     one = jnp.ones((CHUNK, 128), bf16)
     state = jnp.zeros((2 * FEAT, 256), f32)
-    count = q_ref.shape[0] // CHUNK
+    count = kv_ref.shape[0] // CHUNK
     sl = [slice(c * CHUNK, (c + 1) * CHUNK) for c in range(count)]
     for g in range(0, count, TOGETHER):
         cs = range(g, min(g + TOGETHER, count))
-        lq = [dot(lanes(*[q_ref[sl[c], :]] * 2), wq, NT) for c in cs]
         lk = [dot(lanes(*[kv_ref[sl[c], :HD]] * 2), wk, NT) for c in cs]
         fk = [phi(x) for x in lk]
-        fq = [phi(x) for x in lq]
         add = [dot(f.astype(bf16), lanes(kv_ref[sl[c], HD:], one), TN) for f, c in zip(fk, cs)]
         for i, c in enumerate(cs):
-            fq_s[sl[c], :] = fq[i]
             fk_s[sl[c], :] = fk[i]
             st_s[c] = state.astype(bf16)
             state = state + add[i]
 
 
 def assemble(mine, pieces, kv_ref):
-    tok = pieces[0].shape[1]
-    y, core = mine // 4, mine % 2
-    spans = len(pieces) // 2
-    for side in range(2):
-        c = core if side == 0 else 1 - core
-        for d in range(spans):
-            from_y = (y + spans - d) % spans
-            for z in range(2):
-                at = pl.multiple_of((from_y * 4 + z * 2 + c) * tok, tok)
-                kv_ref[pl.ds(at, tok), :] = pieces[side * spans + d][z]
-
-
-def layer_kernel(mine_ref, q_ref, *refs):
-    *pieces, wq_ref, wk_ref, gq_ref, gk_ref, kv_s, o_s, score, fq_s, fk_s, st_s = refs
+    tok = pieces[0].shape[0]
+    y, z, core = mine // 4, mine // 2 % 2, mine % 2
+    spans = len(pieces) // 4
+    for n, piece in enumerate(pieces):
+        side, d = divmod(n, spans)
+        from_y = (y + spans - d) % spans
+        from_z = z if side % 2 == 0 else 1 - z
+        from_core = core if side < 2 else 1 - core
+        at = pl.multiple_of((from_y * 4 + from_z * 2 + from_core) * tok, tok)
+        kv_ref[pl.ds(at, tok), :] = piece[...]
+
+
+def layer_kernel(mine_ref, q_ref, fq_s, *refs):
+    *pieces, wk_ref, gq_ref, gk_ref, kv_s, o_s, score, fk_s, st_s = refs
     assemble(mine_ref[0], pieces, kv_s)
-    features(q_ref, kv_s, signed_pair(wq_ref[0]), signed_pair(wk_ref[0]), fq_s, fk_s, st_s)
+    key_features(kv_s, signed_pair(wk_ref[0]), fk_s, st_s)
     teach(q_ref, kv_s, o_s, score, CHUNK)
     learn(q_ref, kv_s, o_s, fq_s, fk_s, st_s, gq_ref, gk_ref)
 
 
-def layer(mine, q, pieces, wq, wk):
+def layer(mine, q, fq, pieces, wk):
     total = q.shape[0]
     out = [jax.ShapeDtypeStruct((FEAT, HD), f32)] * 2
     return pl.pallas_call(
@@ -231,21 +261,20 @@
         grid_spec=pltpu.PrefetchScalarGridSpec(
             num_scalar_prefetch=1,
             grid=(1,),
-            in_specs=[whole(q)] + [whole(a) for a in pieces] + [head_block(wq), head_block(wk)],
+            in_specs=[IN_VMEM] * (2 + len(pieces)) + [head_block(wk)],
             out_specs=[whole(o) for o in out],
             scratch_shapes=[
                 pltpu.VMEM((total, 2 * HD), bf16),
                 pltpu.VMEM((total, HD), bf16),
                 pltpu.VMEM((2, CHUNK, total), f32),
                 pltpu.VMEM((total, 2 * FEAT), f32),
-                pltpu.VMEM((total, 2 * FEAT), f32),
                 pltpu.VMEM((total // CHUNK, 2 * FEAT, 256), bf16),
             ],
         ),
         out_shape=out,
-        compiler_params=pltpu.CompilerParams(vmem_limit_bytes=56 << 20),
+        compiler_params=pltpu.CompilerParams(vmem_limit_bytes=48 << 20),
         name="layer",
-    )(mine, q, *pieces, wq, wk)
+    )(mine, *(in_vmem(a) for a in (q, fq, *pieces)), wk)
 
 
 def step(x, move):
@@ -257,22 +286,16 @@
     peers = lax.axis_size("seq")
     mine = lax.axis_index("seq")
     here = lanes(keys, values)
-    over = step(here, lambda i: i ^ 2)
-    low = mine // 2 % 2 == 0
-    pair = jnp.stack([jnp.where(low, here, over), jnp.where(low, over, here)])
-    up = lambda x: step(x, lambda i: (i + 4) % peers)
-    down = lambda x: step(x, lambda i: (i - 4) % peers)
-    pieces = [pair] + [step(pair, lambda i, d=d: (i + 4 * d) % peers) for d in range(1, peers // 4)]
-    pieces = pieces + [step(x, lambda i: i ^ 1) for x in pieces]
+    pieces = [here] + [step(here, lambda i, d=d: (i + 4 * d) % peers) for d in range(1, peers // 4)]
+    over = [step(x, lambda i: i ^ 2) for x in pieces]
     qs = queries.reshape(tok, peers, HD).transpose(1, 0, 2)
     q = lax.all_to_all(qs, "seq", 0, 0, tiled=True).reshape(peers * tok, HD)
-    gq, gk = layer(
-        mine.astype(jnp.int32).reshape(1),
-        q,
-        pieces,
-        query_map.transpose(0, 2, 1),
-        key_map.transpose(0, 2, 1),
-    )
+    index = mine.astype(jnp.int32).reshape(1)
+    fq = query_features(index, q, query_map.transpose(0, 2, 1))
+    fq, over[-1] = lax.optimization_barrier((fq, over[-1]))
+    pieces = pieces + over
+    pieces = pieces + [step(x, lambda i: i ^ 1) for x in pieces]
+    gq, gk = layer(index, q, fq, pieces, key_map.transpose(0, 2, 1))
     return gq.T[None], gk.T[None]
 
 

time: 67.8 us -> 65.6 us (0.968)
  waiting for transfers between devices: 20 us -> 13.5 us
  starting transfers between devices: 16.3 us -> 19.8 us
  Pallas kernels: 26.5 us -> 28.1 us
  local copies, waits for them, and re-layouts: 3.91 us -> 3.16 us
    ppermute x8 -> x15, waiting for transfers between devices: 20 us -> 13.5 us  [step(): lax.ppermute(x, 'seq', [(i, move(i)) for i in range(lax.axis_size('seq'))])]
    pallas_call x0 -> x1, Pallas kernels: none -> 3.14 us  [query_features(): pl.pallas_call(query_features_kernel, grid_spec=pltpu.PrefetchScalarGridS...]
    all_to_all x1, starting transfers between devices: 5.44 us -> 7.34 us  [shards(): q = lax.all_to_all(qs, 'seq', 0, 0, tiled=True).reshape(peers * tok, HD)]
    ppermute x8 -> x15, starting transfers between devices: 10.9 us -> 12.5 us  [step(): lax.ppermute(x, 'seq', [(i, move(i)) for i in range(lax.axis_size('seq'))])]
    pallas_call x1, Pallas kernels: 26.5 us -> 25 us  [layer(): pl.pallas_call(layer_kernel, grid_spec=pltpu.PrefetchScalarGridSpec(num_s...]
    unnamed x21 -> x15, local copies, waits for them, and re-layouts: 2.64 us -> 1.88 us
  transfers between devices with their start and end apart: 9 -> 16, of which waited for: 3 -> 4; matrix products, arithmetic and copies ran while one was open for 2% -> 0% of each run, Pallas kernels for 0% -> 5%
where the time goes in v2:
time: 65.6 us; the launch traced here: 65.3 us
  Pallas kernels  28.1 us (43%)
  starting transfers between devices  19.8 us (30%)
  waiting for transfers between devices  13.5 us (21%)
  local copies, waits for them, and re-layouts  3.16 us (5%)
  between operations  0.73 us (1%)
    pallas_call x1, Pallas kernels, layer(): pl.pallas_call(layer_kernel, grid_spec=pltpu.PrefetchScalarGridSpec(num_s...  25 us
    ppermute x15, waiting for transfers between devices, step(): lax.ppermute(x, 'seq', [(i, move(i)) for i in range(lax.axis_size('seq'))])  13.5 us
    ppermute x15, starting transfers between devices, step(): lax.ppermute(x, 'seq', [(i, move(i)) for i in range(lax.axis_size('seq'))])  12.5 us
    all_to_all x1, starting transfers between devices, shards(): q = lax.all_to_all(qs, 'seq', 0, 0, tiled=True).reshape(peers * tok, HD)  7.34 us
    pallas_call x1, Pallas kernels, query_features(): pl.pallas_call(query_features_kernel, grid_spec=pltpu.PrefetchScalarGridS...  3.14 us
    unnamed x15, local copies, waits for them, and re-layouts  1.88 us
  transfers between devices with their start and end apart: 16, of which 4 were waited for; matrix products, arithmetic and copies ran while one was open for 0% of the time, Pallas kernels for 5%

profile of v2, /device:TPU:1, one launch (start us, length us, event | category | flops | bytes accessed | tf_op | source)
XLA Modules:
  0.0 65.3 jit_solution(5579797993550386912)
XLA Ops:
  0.6 0.0 copy-start
  0.6 0.0 copy-start.5
  0.7 0.0 copy-start.6
  0.7 0.0 copy-start.2
  0.7 1.2 %copy-done = bf16[256,2048]{1,0:T(8,128)(2,1)S(1)} copy-done((bf16[256,2048]{1,0:T(8,128)(2,1)S(1)}, bf16[256,2048]{1,0:T(8,128)(2,1)}, u32[]{:S(2)}) %copy-start) | copy-done | bytes 1048600
  1.9 1.3 %bitcast_bitcast_fusion = bf16[16,256,128]{2,1,0:T(8,128)(2,1)} fusion(bf16[256,2048]{1,0:T(8,128)(2,1)S(1)} %copy-done), kind=kLoop, calls=%fused_computation | loop fusion | bytes 2097152 | tf_op jit(solution)/shard_map/transpose | solution.py:291
  3.1 7.3 %all-to-all-start = ((bf16[16,256,128]{2,1,0:T(8,128)(2,1)}), bf16[16,256,128]{2,1,0:T(8,128)(2,1)S(1)}, u32[]{:S(2)}, u32[]{:S(2)}) async-start(bf16[16,256,128]{2,1,0:T(8,128)(2,1)} %bitcast_bitcast_fusion), calls=%async_computation | async-start | bytes 2097152 | tf_op jit(solution)/shard_map/all_to_all | solution.py:292
  10.5 0.0 copy-done.5
  10.5 0.0 copy-start.1
  10.5 0.0 copy-done.6
  10.5 2.7 %collective-permute-start = (bf16[256,256]{1,0:T(8,128)(2,1)S(1)}, bf16[256,256]{1,0:T(8,128)(2,1)S(1)}, u32[]{:S(2)}, u32[]{:S(2)}) collective-permute-start(bf16[256,256]{1,0:T(8,128)(2,1)S(1)} %constant_dynamic-update-slice_fusion.refs_0_), channel_id=1, source_target_pairs={{0,12},{1,13},{2,14},{3,15},{4,0},{5,1},{6,2},{7,3},{8,4},{9,5},{1... | collective-permute-start | bytes 393224 | tf_op jit(solution)/shard_map/ppermute | solution.py:281
  13.2 1.2 %collective-permute-start.4 = (bf16[256,256]{1,0:T(8,128)(2,1)S(1)}, bf16[256,256]{1,0:T(8,128)(2,1)S(1)}, u32[]{:S(2)}, u32[]{:S(2)}) collective-permute-start(bf16[256,256]{1,0:T(8,128)(2,1)S(1)} %constant_dynamic-update-slice_fusion.refs_0_), channel_id=1, source_target_pairs={{0,2},{1,3},{2,0},{3,1},{4,6},{5,7},{6,4},{7,5},{8,10},{9,11},{10,... | collective-permute-start | bytes 393224 | tf_op jit(solution)/shard_map/ppermute | solution.py:281
  14.4 0.6 collective-permute-start.3
  15.0 0.6 collective-permute-start.2
  15.5 11.5 %collective-permute-done.refs_3_ = bf16[256,256]{1,0:T(8,128)(2,1)S(1)} collective-permute-done((bf16[256,256]{1,0:T(8,128)(2,1)S(1)}, bf16[256,256]{1,0:T(8,128)(2,1)S(1)}, u32[]{:S(2)}, u32[]{:S(2)}) %collective-permute-start) | collective-permute-done | bytes 131104 | tf_op jit(solution)/shard_map/ppermute | solution.py:281
  27.1 1.2 %collective-permute-start.1 = (bf16[256,256]{1,0:T(8,128)(2,1)S(1)}, bf16[256,256]{1,0:T(8,128)(2,1)S(1)}, u32[]{:S(2)}, u32[]{:S(2)}) collective-permute-start(bf16[256,256]{1,0:T(8,128)(2,1)S(1)} %collective-permute-done.refs_3_), channel_id=1, source_target_pairs={{0,2},{1,3},{2,0},{3,1},{4,6},{5,7},{6,4},{7,5},{8,10},{9,11},{10,... | collective-permute-start | bytes 393224 | tf_op jit(solution)/shard_map/ppermute | solution.py:281
  28.2 1.5 %collective-permute-start.7 = (bf16[256,256]{1,0:T(8,128)(2,1)S(1)}, bf16[256,256]{1,0:T(8,128)(2,1)}, u32[]{:S(2)}, u32[]{:S(2)}) collective-permute-start(bf16[256,256]{1,0:T(8,128)(2,1)S(1)} %constant_dynamic-update-slice_fusion.refs_0_), channel_id=1, source_target_pairs={{0,1},{1,0},{2,3},{3,2},{4,5},{5,4},{6,7},{7,6},{8,9},{9,8},{10,11... | collective-permute-start | bytes 393224 | tf_op jit(solution)/shard_map/ppermute | solution.py:281
  29.8 0.0 collective-permute-done.4.refs_4_
  29.8 0.0 collective-permute-start.11
  29.8 0.0 collective-permute-done.3.refs_2_
  29.8 0.4 collective-permute-start.6
  30.1 0.9 %collective-permute-done.2.refs_1_ = bf16[256,256]{1,0:T(8,128)(2,1)} collective-permute-done((bf16[256,256]{1,0:T(8,128)(2,1)S(1)}, bf16[256,256]{1,0:T(8,128)(2,1)}, u32[]{:S(2)}, u32[]{:S(2)}) %collective-permute-start.2) | collective-permute-done | bytes 131104 | tf_op jit(solution)/shard_map/ppermute | solution.py:281
  31.0 1.2 %collective-permute-start.5 = (bf16[256,256]{1,0:T(8,128)(2,1)}, bf16[256,256]{1,0:T(8,128)(2,1)}, u32[]{:S(2)}, u32[]{:S(2)}) collective-permute-start(bf16[256,256]{1,0:T(8,128)(2,1)} %collective-permute-done.2.refs_1_), channel_id=1, source_target_pairs={{0,2},{1,3},{2,0},{3,1},{4,6},{5,7},{6,4},{7,5},{8,10},{9,11},{10,... | collective-permute-start | bytes 393224 | tf_op jit(solution)/shard_map/ppermute | solution.py:281
  32.2 0.0 collective-permute-done.1.refs_7_
  32.2 0.0 copy-start.3
  32.2 0.7 copy-done.3
  32.8 1.2 %collective-permute-start.9 = (bf16[256,256]{1,0:T(8,128)(2,1)}, bf16[256,256]{1,0:T(8,128)(2,1)}, u32[]{:S(2)}, u32[]{:S(2)}) collective-permute-start(bf16[256,256]{1,0:T(8,128)(2,1)} %collective-permute-done.3.refs_2_), channel_id=1, source_target_pairs={{0,1},{1,0},{2,3},{3,2},{4,5},{5,4},{6,7},{7,6},{8,9},{9,8},{10,11... | collective-permute-start | bytes 393224 | tf_op jit(solution)/shard_map/ppermute | solution.py:281
  34.0 0.0 all-to-all-done
  34.0 0.0 copy-done.2
  34.0 3.1 %query_features.1.fq_s = f32[4096,128]{1,0:T(8,128)S(1)} custom-call(s32[1]{0:T(128)} %bitcast.mine_ref, bf16[4096,128]{1,0:T(8,128)(2,1)S(1)} %bitcast.17, f32[16,64,128]{2,1,0:T(8,128)S(1)} %bitcast.20), custom_call_target="tpu_custom_call" | custom-call | tf_op jit(solution)/shard_map/query_features/pallas_call | solution.py:205
  37.1 0.0 collective-permute-done.7.refs_8_
  37.2 0.1 collective-permute-start.8
  37.3 0.0 collective-permute-done.11.refs_12_
  37.3 0.5 collective-permute-start.10
  37.7 0.0 collective-permute-done.6.refs_6_
  37.7 0.1 collective-permute-start.13
  37.8 0.0 collective-permute-done.5.refs_5_
  37.9 1.1 %collective-permute-start.12 = (bf16[256,256]{1,0:T(8,128)(2,1)}, bf16[256,256]{1,0:T(8,128)(2,1)S(1)}, u32[]{:S(2)}, u32[]{:S(2)}) collective-permute-start(bf16[256,256]{1,0:T(8,128)(2,1)} %collective-permute-done.5.refs_5_), channel_id=1, source_target_pairs={{0,1},{1,0},{2,3},{3,2},{4,5},{5,4},{6,7},{7,6},{8,9},{9,8},{10,11... | collective-permute-start | bytes 393224 | tf_op jit(solution)/shard_map/ppermute | solution.py:281
  39.0 0.0 collective-permute-done.9.refs_10_
  39.0 0.0 copy-done.4
  39.0 0.3 collective-permute-start.14
  39.3 0.0 collective-permute-done.8.refs_9_
  39.3 0.0 collective-permute-done.10.refs_11_
  39.3 0.0 collective-permute-done.13.refs_14_
  39.3 0.9 %collective-permute-done.12.refs_13_ = bf16[256,256]{1,0:T(8,128)(2,1)S(1)} collective-permute-done((bf16[256,256]{1,0:T(8,128)(2,1)}, bf16[256,256]{1,0:T(8,128)(2,1)S(1)}, u32[]{:S(2)}, u32[]{:S(2)}) %collective-permute-start.12) | collective-permute-done | bytes 131104 | tf_op jit(solution)/shard_map/ppermute | solution.py:281
  40.2 0.2 collective-permute-done.14.refs_15_
  40.4 0.0 copy-done.1
  40.4 25.0 %layer.1 = (f32[64,128]{1,0:T(8,128)}, f32[64,128]{1,0:T(8,128)}) custom-call(s32[1]{0:T(128)} %bitcast.mine_ref, bf16[4096,128]{1,0:T(8,128)(2,1)S(1)} %bitcast.18, f32[4096,128]{1,0:T(8,128)S(1)} %query_features.1.fq_s, bf16[256,256]{1,0:T(8,128)(2,1)S(1)} %constant_dynamic-update-slice_fusion.refs_0_, bf16[256,256]{1,0:T(8,128)(2,1)} %collective-permute-done.2.refs_1_, ...), custom_call_target="tpu_custom_call" | custom-call | tf_op jit(solution)/shard_map/layer/pallas_call | solution.py:259
  (3 shorter events, 0.0 us)
Async XLA Ops:
  0.6 1.2 %copy-start = (bf16[256,2048]{1,0:T(8,128)(2,1)S(1)}, bf16[256,2048]{1,0:T(8,128)(2,1)}, u32[]{:S(2)}) copy-start(bf16[256,2048]{1,0:T(8,128)(2,1)} %param.5) | copy-start | bytes 3145732
  0.6 9.8 %copy-start.5 = (bf16[256,128]{1,0:T(8,128)(2,1)S(1)}, bf16[256,128]{1,0:T(8,128)(2,1)}, u32[]{:S(2)}) copy-start(bf16[256,128]{1,0:T(8,128)(2,1)} %param.6) | copy-start | bytes 196612
  0.7 9.9 %copy-start.6 = (bf16[256,128]{1,0:T(8,128)(2,1)S(1)}, bf16[256,128]{1,0:T(8,128)(2,1)}, u32[]{:S(2)}) copy-start(bf16[256,128]{1,0:T(8,128)(2,1)} %param.7) | copy-start | bytes 196612
  0.7 33.3 %copy-start.2 = (f32[16,128,64]{1,2,0:T(8,128)S(1)}, f32[16,128,64]{1,2,0:T(8,128)}, u32[]{:S(2)}) copy-start(f32[16,128,64]{1,2,0:T(8,128)} %param.8) | copy-start | bytes 1572868
  3.1 30.9 %all-to-all-start = ((bf16[16,256,128]{2,1,0:T(8,128)(2,1)}), bf16[16,256,128]{2,1,0:T(8,128)(2,1)S(1)}, u32[]{:S(2)}, u32[]{:S(2)}) async-start(bf16[16,256,128]{2,1,0:T(8,128)(2,1)} %bitcast_bitcast_fusion), calls=%async_computation | async-start | bytes 2097152 | tf_op jit(solution)/shard_map/all_to_all | solution.py:292
  10.5 29.9 %copy-start.1 = (f32[16,128,64]{1,2,0:T(8,128)S(1)}, f32[16,128,64]{1,2,0:T(8,128)}, u32[]{:S(2)}) copy-start(f32[16,128,64]{1,2,0:T(8,128)} %param.9) | copy-start | bytes 1572868
  10.5 16.5 %collective-permute-start = (bf16[256,256]{1,0:T(8,128)(2,1)S(1)}, bf16[256,256]{1,0:T(8,128)(2,1)S(1)}, u32[]{:S(2)}, u32[]{:S(2)}) collective-permute-start(bf16[256,256]{1,0:T(8,128)(2,1)S(1)} %constant_dynamic-update-slice_fusion.refs_0_), channel_id=1, source_target_pairs={{0,12},{1,13},{2,14},{3,15},{4,0},{5,1},{6,2},{7,3},{8,4},{9,5},{1... | collective-permute-start | bytes 393224 | tf_op jit(solution)/shard_map/ppermute | solution.py:281
  13.2 16.6 %collective-permute-start.4 = (bf16[256,256]{1,0:T(8,128)(2,1)S(1)}, bf16[256,256]{1,0:T(8,128)(2,1)S(1)}, u32[]{:S(2)}, u32[]{:S(2)}) collective-permute-start(bf16[256,256]{1,0:T(8,128)(2,1)S(1)} %constant_dynamic-update-slice_fusion.refs_0_), channel_id=1, source_target_pairs={{0,2},{1,3},{2,0},{3,1},{4,6},{5,7},{6,4},{7,5},{8,10},{9,11},{10,... | collective-permute-start | bytes 393224 | tf_op jit(solution)/shard_map/ppermute | solution.py:281
  14.4 15.4 %collective-permute-start.3 = (bf16[256,256]{1,0:T(8,128)(2,1)S(1)}, bf16[256,256]{1,0:T(8,128)(2,1)}, u32[]{:S(2)}, u32[]{:S(2)}) collective-permute-start(bf16[256,256]{1,0:T(8,128)(2,1)S(1)} %constant_dynamic-update-slice_fusion.refs_0_), channel_id=1, source_target_pairs={{0,8},{1,9},{2,10},{3,11},{4,12},{5,13},{6,14},{7,15},{8,0},{9,1},... | collective-permute-start | bytes 393224 | tf_op jit(solution)/shard_map/ppermute | solution.py:281
  15.0 16.0 %collective-permute-start.2 = (bf16[256,256]{1,0:T(8,128)(2,1)S(1)}, bf16[256,256]{1,0:T(8,128)(2,1)}, u32[]{:S(2)}, u32[]{:S(2)}) collective-permute-start(bf16[256,256]{1,0:T(8,128)(2,1)S(1)} %constant_dynamic-update-slice_fusion.refs_0_), channel_id=1, source_target_pairs={{0,4},{1,5},{2,6},{3,7},{4,8},{5,9},{6,10},{7,11},{8,12},{9,13},{1... | collective-permute-start | bytes 393224 | tf_op jit(solution)/shard_map/ppermute | solution.py:281
  27.1 5.1 %collective-permute-start.1 = (bf16[256,256]{1,0:T(8,128)(2,1)S(1)}, bf16[256,256]{1,0:T(8,128)(2,1)S(1)}, u32[]{:S(2)}, u32[]{:S(2)}) collective-permute-start(bf16[256,256]{1,0:T(8,128)(2,1)S(1)} %collective-permute-done.refs_3_), channel_id=1, source_target_pairs={{0,2},{1,3},{2,0},{3,1},{4,6},{5,7},{6,4},{7,5},{8,10},{9,11},{10,... | collective-permute-start | bytes 393224 | tf_op jit(solution)/shard_map/ppermute | solution.py:281
  28.2 8.9 %collective-permute-start.7 = (bf16[256,256]{1,0:T(8,128)(2,1)S(1)}, bf16[256,256]{1,0:T(8,128)(2,1)}, u32[]{:S(2)}, u32[]{:S(2)}) collective-permute-start(bf16[256,256]{1,0:T(8,128)(2,1)S(1)} %constant_dynamic-update-slice_fusion.refs_0_), channel_id=1, source_target_pairs={{0,1},{1,0},{2,3},{3,2},{4,5},{5,4},{6,7},{7,6},{8,9},{9,8},{10,11... | collective-permute-start | bytes 393224 | tf_op jit(solution)/shard_map/ppermute | solution.py:281
  29.8 7.5 %collective-permute-start.11 = (bf16[256,256]{1,0:T(8,128)(2,1)S(1)}, bf16[256,256]{1,0:T(8,128)(2,1)}, u32[]{:S(2)}, u32[]{:S(2)}) collective-permute-start(bf16[256,256]{1,0:T(8,128)(2,1)S(1)} %collective-permute-done.4.refs_4_), channel_id=1, source_target_pairs={{0,1},{1,0},{2,3},{3,2},{4,5},{5,4},{6,7},{7,6},{8,9},{9,8},{10,11... | collective-permute-start | bytes 393224 | tf_op jit(solution)/shard_map/ppermute | solution.py:281
  29.8 8.0 %collective-permute-start.6 = (bf16[256,256]{1,0:T(8,128)(2,1)}, bf16[256,256]{1,0:T(8,128)(2,1)}, u32[]{:S(2)}, u32[]{:S(2)}) collective-permute-start(bf16[256,256]{1,0:T(8,128)(2,1)} %collective-permute-done.3.refs_2_), channel_id=1, source_target_pairs={{0,2},{1,3},{2,0},{3,1},{4,6},{5,7},{6,4},{7,5},{8,10},{9,11},{10,... | collective-permute-start | bytes 393224 | tf_op jit(solution)/shard_map/ppermute | solution.py:281
  31.0 6.9 %collective-permute-start.5 = (bf16[256,256]{1,0:T(8,128)(2,1)}, bf16[256,256]{1,0:T(8,128)(2,1)}, u32[]{:S(2)}, u32[]{:S(2)}) collective-permute-start(bf16[256,256]{1,0:T(8,128)(2,1)} %collective-permute-done.2.refs_1_), channel_id=1, source_target_pairs={{0,2},{1,3},{2,0},{3,1},{4,6},{5,7},{6,4},{7,5},{8,10},{9,11},{10,... | collective-permute-start | bytes 393224 | tf_op jit(solution)/shard_map/ppermute | solution.py:281
  32.2 0.7 copy-start.3
  32.8 6.2 %collective-permute-start.9 = (bf16[256,256]{1,0:T(8,128)(2,1)}, bf16[256,256]{1,0:T(8,128)(2,1)}, u32[]{:S(2)}, u32[]{:S(2)}) collective-permute-start(bf16[256,256]{1,0:T(8,128)(2,1)} %collective-permute-done.3.refs_2_), channel_id=1, source_target_pairs={{0,1},{1,0},{2,3},{3,2},{4,5},{5,4},{6,7},{7,6},{8,9},{9,8},{10,11... | collective-permute-start | bytes 393224 | tf_op jit(solution)/shard_map/ppermute | solution.py:281
  34.0 5.0 %copy-start.4 = (bf16[256,256]{1,0:T(8,128)(2,1)S(1)}, bf16[256,256]{1,0:T(8,128)(2,1)}, u32[]{:S(2)}) copy-start(bf16[256,256]{1,0:T(8,128)(2,1)} %copy-done.3) | copy-start | bytes 393220
  37.2 2.1 %collective-permute-start.8 = (bf16[256,256]{1,0:T(8,128)(2,1)}, bf16[256,256]{1,0:T(8,128)(2,1)S(1)}, u32[]{:S(2)}, u32[]{:S(2)}) collective-permute-start(bf16[256,256]{1,0:T(8,128)(2,1)} %collective-permute-done.2.refs_1_), channel_id=1, source_target_pairs={{0,1},{1,0},{2,3},{3,2},{4,5},{5,4},{6,7},{7,6},{8,9},{9,8},{10,11... | collective-permute-start | bytes 393224 | tf_op jit(solution)/shard_map/ppermute | solution.py:281
  37.3 2.0 %collective-permute-start.10 = (bf16[256,256]{1,0:T(8,128)(2,1)S(1)}, bf16[256,256]{1,0:T(8,128)(2,1)S(1)}, u32[]{:S(2)}, u32[]{:S(2)}) collective-permute-start(bf16[256,256]{1,0:T(8,128)(2,1)S(1)} %collective-permute-done.refs_3_), channel_id=1, source_target_pairs={{0,1},{1,0},{2,3},{3,2},{4,5},{5,4},{6,7},{7,6},{8,9},{9,8},{10,11... | collective-permute-start | bytes 393224 | tf_op jit(solution)/shard_map/ppermute | solution.py:281
  37.7 1.6 %collective-permute-start.13 = (bf16[256,256]{1,0:T(8,128)(2,1)}, bf16[256,256]{1,0:T(8,128)(2,1)S(1)}, u32[]{:S(2)}, u32[]{:S(2)}) collective-permute-start(bf16[256,256]{1,0:T(8,128)(2,1)} %collective-permute-done.6.refs_6_), channel_id=1, source_target_pairs={{0,1},{1,0},{2,3},{3,2},{4,5},{5,4},{6,7},{7,6},{8,9},{9,8},{10,11... | collective-permute-start | bytes 393224 | tf_op jit(solution)/shard_map/ppermute | solution.py:281
  37.9 2.3 %collective-permute-start.12 = (bf16[256,256]{1,0:T(8,128)(2,1)}, bf16[256,256]{1,0:T(8,128)(2,1)S(1)}, u32[]{:S(2)}, u32[]{:S(2)}) collective-permute-start(bf16[256,256]{1,0:T(8,128)(2,1)} %collective-permute-done.5.refs_5_), channel_id=1, source_target_pairs={{0,1},{1,0},{2,3},{3,2},{4,5},{5,4},{6,7},{7,6},{8,9},{9,8},{10,11... | collective-permute-start | bytes 393224 | tf_op jit(solution)/shard_map/ppermute | solution.py:281
  39.0 1.4 %collective-permute-start.14 = (bf16[256,256]{1,0:T(8,128)(2,1)S(1)}, bf16[256,256]{1,0:T(8,128)(2,1)S(1)}, u32[]{:S(2)}, u32[]{:S(2)}) collective-permute-start(bf16[256,256]{1,0:T(8,128)(2,1)S(1)} %copy-done.4), channel_id=1, source_target_pairs={{0,1},{1,0},{2,3},{3,2},{4,5},{5,4},{6,7},{7,6},{8,9},{9,8},{10,11... | collective-permute-start | bytes 393224 | tf_op jit(solution)/shard_map/ppermute | solution.py:281

commit v3 on v2

--- a/solution.py
+++ b/solution.py
@@ -153,22 +153,20 @@
         dd = [split(jnp.sum(dn[i] * out[i], axis=1, keepdims=True) * (-1.0 / 64)) for i in every]
         dd = [jnp.where(first_half((CHUNK, 128)), h.astype(f32), l.astype(f32)).astype(bf16) for h, l in dd]
         dx = [lanes(dn[i].astype(bf16), dd[i]) for i in every]
-        da, dat = [], []
+        da = []
         for i in every:
-            a, b = dot(dx[i], ve[i], NT), dot(ve[i], dx[i], NT)
+            a = dot(dx[i], ve[i], NT)
             if cs[i] == 0:
-                low = split(dn[i])[1]
-                a, b = a + dot(low, ve[i][:, :HD], NT), b + dot(ve[i][:, :HD], low, NT)
+                a = a + dot(split(dn[i])[1], ve[i][:, :HD], NT)
             da.append(split(jnp.where(r >= k, a, 0.0)))
-            dat.append(split(jnp.where(r <= k, b, 0.0)))
         after = []
         for i in every:
             after.append(later.astype(bf16))
             later = later + dot(fq[i][0], dx[i], TN)
         x = [dot(da[i][0], lanes(*fk[i])) for i in every]
         dfq = [x[i][:, :128] + x[i][:, 128:] + dot(da[i][1], fk[i][0]) + dot(dx[i], st[i], NT) for i in every]
-        x = [dot(dat[i][0], lanes(*fq[i])) for i in every]
-        dfk = [x[i][:, :128] + x[i][:, 128:] + dot(dat[i][1], fq[i][0]) + dot(ve[i], after[i], NT) for i in every]
+        x = [dot(da[i][0], lanes(*fq[i]), TN) for i in every]
+        dfk = [x[i][:, :128] + x[i][:, 128:] + dot(da[i][1], fq[i][0], TN) + dot(ve[i], after[i], NT) for i in every]
         yq = [lanes(*split(phi_back(fq_s[sl[cs[i]], :], dfq[i]))) for i in every]
         yk = [lanes(*split(phi_back(fk_s[sl[cs[i]], :], dfk[i]))) for i in every]
         lo, hi = sl[cs[-1]].start, sl[cs[0]].stop

time: 65.6 us -> 64.7 us (0.986)
  Pallas kernels: 28.1 us -> 27.2 us
    pallas_call x1, Pallas kernels: 25 us -> 24.1 us  [layer(): pl.pallas_call(layer_kernel, grid_spec=pltpu.PrefetchScalarGridSpec(num_s...]
where the time goes in v3:
time: 64.7 us; the launch traced here: 64.5 us
  Pallas kernels  27.2 us (42%)
  starting transfers between devices  19.8 us (31%)
  waiting for transfers between devices  13.5 us (21%)
  local copies, waits for them, and re-layouts  3.16 us (5%)
  between operations  0.73 us (1%)
    pallas_call x1, Pallas kernels, layer(): pl.pallas_call(layer_kernel, grid_spec=pltpu.PrefetchScalarGridSpec(num_s...  24.1 us
    ppermute x15, waiting for transfers between devices, step(): lax.ppermute(x, 'seq', [(i, move(i)) for i in range(lax.axis_size('seq'))])  13.5 us
    ppermute x15, starting transfers between devices, step(): lax.ppermute(x, 'seq', [(i, move(i)) for i in range(lax.axis_size('seq'))])  12.5 us
    all_to_all x1, starting transfers between devices, shards(): q = lax.all_to_all(qs, 'seq', 0, 0, tiled=True).reshape(peers * tok, HD)  7.34 us
    pallas_call x1, Pallas kernels, query_features(): pl.pallas_call(query_features_kernel, grid_spec=pltpu.PrefetchScalarGridS...  3.14 us
    unnamed x15, local copies, waits for them, and re-layouts  1.88 us
  transfers between devices with their start and end apart: 16, of which 4 were waited for; matrix products, arithmetic and copies ran while one was open for 0% of the time, Pallas kernels for 5%

profile of v3, /device:TPU:1, one launch (start us, length us, event | category | flops | bytes accessed | tf_op | source)
XLA Modules:
  0.0 64.5 jit_solution(9629311339839976996)
XLA Ops:
  0.6 0.0 copy-start
  0.6 0.0 copy-start.5
  0.7 0.0 copy-start.6
  0.7 0.0 copy-start.2
  0.7 1.2 %copy-done = bf16[256,2048]{1,0:T(8,128)(2,1)S(1)} copy-done((bf16[256,2048]{1,0:T(8,128)(2,1)S(1)}, bf16[256,2048]{1,0:T(8,128)(2,1)}, u32[]{:S(2)}) %copy-start) | copy-done | bytes 1048600
  1.9 1.3 %bitcast_bitcast_fusion = bf16[16,256,128]{2,1,0:T(8,128)(2,1)} fusion(bf16[256,2048]{1,0:T(8,128)(2,1)S(1)} %copy-done), kind=kLoop, calls=%fused_computation | loop fusion | bytes 2097152 | tf_op jit(solution)/shard_map/transpose | solution.py:289
  3.1 7.3 %all-to-all-start = ((bf16[16,256,128]{2,1,0:T(8,128)(2,1)}), bf16[16,256,128]{2,1,0:T(8,128)(2,1)S(1)}, u32[]{:S(2)}, u32[]{:S(2)}) async-start(bf16[16,256,128]{2,1,0:T(8,128)(2,1)} %bitcast_bitcast_fusion), calls=%async_computation | async-start | bytes 2097152 | tf_op jit(solution)/shard_map/all_to_all | solution.py:290
  10.5 0.0 copy-done.5
  10.5 0.0 copy-start.1
  10.5 0.0 copy-done.6
  10.5 2.7 %collective-permute-start = (bf16[256,256]{1,0:T(8,128)(2,1)S(1)}, bf16[256,256]{1,0:T(8,128)(2,1)S(1)}, u32[]{:S(2)}, u32[]{:S(2)}) collective-permute-start(bf16[256,256]{1,0:T(8,128)(2,1)S(1)} %constant_dynamic-update-slice_fusion.refs_0_), channel_id=1, source_target_pairs={{0,12},{1,13},{2,14},{3,15},{4,0},{5,1},{6,2},{7,3},{8,4},{9,5},{1... | collective-permute-start | bytes 393224 | tf_op jit(solution)/shard_map/ppermute | solution.py:279
  13.2 1.2 %collective-permute-start.4 = (bf16[256,256]{1,0:T(8,128)(2,1)S(1)}, bf16[256,256]{1,0:T(8,128)(2,1)S(1)}, u32[]{:S(2)}, u32[]{:S(2)}) collective-permute-start(bf16[256,256]{1,0:T(8,128)(2,1)S(1)} %constant_dynamic-update-slice_fusion.refs_0_), channel_id=1, source_target_pairs={{0,2},{1,3},{2,0},{3,1},{4,6},{5,7},{6,4},{7,5},{8,10},{9,11},{10,... | collective-permute-start | bytes 393224 | tf_op jit(solution)/shard_map/ppermute | solution.py:279
  14.4 0.6 collective-permute-start.3
  15.0 0.6 collective-permute-start.2
  15.5 11.5 %collective-permute-done.refs_3_ = bf16[256,256]{1,0:T(8,128)(2,1)S(1)} collective-permute-done((bf16[256,256]{1,0:T(8,128)(2,1)S(1)}, bf16[256,256]{1,0:T(8,128)(2,1)S(1)}, u32[]{:S(2)}, u32[]{:S(2)}) %collective-permute-start) | collective-permute-done | bytes 131104 | tf_op jit(solution)/shard_map/ppermute | solution.py:279
  27.1 1.2 %collective-permute-start.1 = (bf16[256,256]{1,0:T(8,128)(2,1)S(1)}, bf16[256,256]{1,0:T(8,128)(2,1)S(1)}, u32[]{:S(2)}, u32[]{:S(2)}) collective-permute-start(bf16[256,256]{1,0:T(8,128)(2,1)S(1)} %collective-permute-done.refs_3_), channel_id=1, source_target_pairs={{0,2},{1,3},{2,0},{3,1},{4,6},{5,7},{6,4},{7,5},{8,10},{9,11},{10,... | collective-permute-start | bytes 393224 | tf_op jit(solution)/shard_map/ppermute | solution.py:279
  28.2 1.5 %collective-permute-start.7 = (bf16[256,256]{1,0:T(8,128)(2,1)S(1)}, bf16[256,256]{1,0:T(8,128)(2,1)}, u32[]{:S(2)}, u32[]{:S(2)}) collective-permute-start(bf16[256,256]{1,0:T(8,128)(2,1)S(1)} %constant_dynamic-update-slice_fusion.refs_0_), channel_id=1, source_target_pairs={{0,1},{1,0},{2,3},{3,2},{4,5},{5,4},{6,7},{7,6},{8,9},{9,8},{10,11... | collective-permute-start | bytes 393224 | tf_op jit(solution)/shard_map/ppermute | solution.py:279
  29.8 0.0 collective-permute-done.4.refs_4_
  29.8 0.0 collective-permute-start.11
  29.8 0.0 collective-permute-done.3.refs_2_
  29.8 0.4 collective-permute-start.6
  30.1 0.9 %collective-permute-done.2.refs_1_ = bf16[256,256]{1,0:T(8,128)(2,1)} collective-permute-done((bf16[256,256]{1,0:T(8,128)(2,1)S(1)}, bf16[256,256]{1,0:T(8,128)(2,1)}, u32[]{:S(2)}, u32[]{:S(2)}) %collective-permute-start.2) | collective-permute-done | bytes 131104 | tf_op jit(solution)/shard_map/ppermute | solution.py:279
  31.0 1.2 %collective-permute-start.5 = (bf16[256,256]{1,0:T(8,128)(2,1)}, bf16[256,256]{1,0:T(8,128)(2,1)}, u32[]{:S(2)}, u32[]{:S(2)}) collective-permute-start(bf16[256,256]{1,0:T(8,128)(2,1)} %collective-permute-done.2.refs_1_), channel_id=1, source_target_pairs={{0,2},{1,3},{2,0},{3,1},{4,6},{5,7},{6,4},{7,5},{8,10},{9,11},{10,... | collective-permute-start | bytes 393224 | tf_op jit(solution)/shard_map/ppermute | solution.py:279
  32.2 0.0 collective-permute-done.1.refs_7_
  32.2 0.0 copy-start.3
  32.2 0.7 %copy-done.3 = bf16[256,256]{1,0:T(8,128)(2,1)} copy-done((bf16[256,256]{1,0:T(8,128)(2,1)}, bf16[256,256]{1,0:T(8,128)(2,1)S(1)}, u32[]{:S(2)}) %copy-start.3) | copy-done | bytes 131096
  32.8 1.2 %collective-permute-start.9 = (bf16[256,256]{1,0:T(8,128)(2,1)}, bf16[256,256]{1,0:T(8,128)(2,1)}, u32[]{:S(2)}, u32[]{:S(2)}) collective-permute-start(bf16[256,256]{1,0:T(8,128)(2,1)} %collective-permute-done.3.refs_2_), channel_id=1, source_target_pairs={{0,1},{1,0},{2,3},{3,2},{4,5},{5,4},{6,7},{7,6},{8,9},{9,8},{10,11... | collective-permute-start | bytes 393224 | tf_op jit(solution)/shard_map/ppermute | solution.py:279
  34.0 0.0 all-to-all-done
  34.0 0.0 copy-done.2
  34.0 3.1 %query_features.1.fq_s = f32[4096,128]{1,0:T(8,128)S(1)} custom-call(s32[1]{0:T(128)} %bitcast.mine_ref, bf16[4096,128]{1,0:T(8,128)(2,1)S(1)} %bitcast.17, f32[16,64,128]{2,1,0:T(8,128)S(1)} %bitcast.20), custom_call_target="tpu_custom_call" | custom-call | tf_op jit(solution)/shard_map/query_features/pallas_call | solution.py:203
  37.1 0.0 collective-permute-done.7.refs_8_
  37.2 0.1 collective-permute-start.8
  37.3 0.0 collective-permute-done.11.refs_12_
  37.3 0.5 collective-permute-start.10
  37.7 0.0 collective-permute-done.6.refs_6_
  37.7 0.1 collective-permute-start.13
  37.8 0.0 collective-permute-done.5.refs_5_
  37.9 1.1 %collective-permute-start.12 = (bf16[256,256]{1,0:T(8,128)(2,1)}, bf16[256,256]{1,0:T(8,128)(2,1)S(1)}, u32[]{:S(2)}, u32[]{:S(2)}) collective-permute-start(bf16[256,256]{1,0:T(8,128)(2,1)} %collective-permute-done.5.refs_5_), channel_id=1, source_target_pairs={{0,1},{1,0},{2,3},{3,2},{4,5},{5,4},{6,7},{7,6},{8,9},{9,8},{10,11... | collective-permute-start | bytes 393224 | tf_op jit(solution)/shard_map/ppermute | solution.py:279
  39.0 0.0 collective-permute-done.9.refs_10_
  39.0 0.0 copy-done.4
  39.0 0.3 collective-permute-start.14
  39.3 0.0 collective-permute-done.8.refs_9_
  39.3 0.0 collective-permute-done.10.refs_11_
  39.3 0.0 collective-permute-done.13.refs_14_
  39.3 0.9 %collective-permute-done.12.refs_13_ = bf16[256,256]{1,0:T(8,128)(2,1)S(1)} collective-permute-done((bf16[256,256]{1,0:T(8,128)(2,1)}, bf16[256,256]{1,0:T(8,128)(2,1)S(1)}, u32[]{:S(2)}, u32[]{:S(2)}) %collective-permute-start.12) | collective-permute-done | bytes 131104 | tf_op jit(solution)/shard_map/ppermute | solution.py:279
  40.2 0.2 collective-permute-done.14.refs_15_
  40.4 0.0 copy-done.1
  40.4 24.1 %layer.1 = (f32[64,128]{1,0:T(8,128)}, f32[64,128]{1,0:T(8,128)}) custom-call(s32[1]{0:T(128)} %bitcast.mine_ref, bf16[4096,128]{1,0:T(8,128)(2,1)S(1)} %bitcast.18, f32[4096,128]{1,0:T(8,128)S(1)} %query_features.1.fq_s, bf16[256,256]{1,0:T(8,128)(2,1)S(1)} %constant_dynamic-update-slice_fusion.refs_0_, bf16[256,256]{1,0:T(8,128)(2,1)} %collective-permute-done.2.refs_1_, ...), custom_call_target="tpu_custom_call" | custom-call | tf_op jit(solution)/shard_map/layer/pallas_call | solution.py:257
  (3 shorter events, 0.0 us)
Async XLA Ops:
  0.6 1.2 %copy-start = (bf16[256,2048]{1,0:T(8,128)(2,1)S(1)}, bf16[256,2048]{1,0:T(8,128)(2,1)}, u32[]{:S(2)}) copy-start(bf16[256,2048]{1,0:T(8,128)(2,1)} %param.5) | copy-start | bytes 3145732
  0.6 9.8 %copy-start.5 = (bf16[256,128]{1,0:T(8,128)(2,1)S(1)}, bf16[256,128]{1,0:T(8,128)(2,1)}, u32[]{:S(2)}) copy-start(bf16[256,128]{1,0:T(8,128)(2,1)} %param.6) | copy-start | bytes 196612
  0.7 9.9 %copy-start.6 = (bf16[256,128]{1,0:T(8,128)(2,1)S(1)}, bf16[256,128]{1,0:T(8,128)(2,1)}, u32[]{:S(2)}) copy-start(bf16[256,128]{1,0:T(8,128)(2,1)} %param.7) | copy-start | bytes 196612
  0.7 33.3 %copy-start.2 = (f32[16,128,64]{1,2,0:T(8,128)S(1)}, f32[16,128,64]{1,2,0:T(8,128)}, u32[]{:S(2)}) copy-start(f32[16,128,64]{1,2,0:T(8,128)} %param.8) | copy-start | bytes 1572868
  3.1 30.9 %all-to-all-start = ((bf16[16,256,128]{2,1,0:T(8,128)(2,1)}), bf16[16,256,128]{2,1,0:T(8,128)(2,1)S(1)}, u32[]{:S(2)}, u32[]{:S(2)}) async-start(bf16[16,256,128]{2,1,0:T(8,128)(2,1)} %bitcast_bitcast_fusion), calls=%async_computation | async-start | bytes 2097152 | tf_op jit(solution)/shard_map/all_to_all | solution.py:290
  10.5 29.9 %copy-start.1 = (f32[16,128,64]{1,2,0:T(8,128)S(1)}, f32[16,128,64]{1,2,0:T(8,128)}, u32[]{:S(2)}) copy-start(f32[16,128,64]{1,2,0:T(8,128)} %param.9) | copy-start | bytes 1572868
  10.5 16.5 %collective-permute-start = (bf16[256,256]{1,0:T(8,128)(2,1)S(1)}, bf16[256,256]{1,0:T(8,128)(2,1)S(1)}, u32[]{:S(2)}, u32[]{:S(2)}) collective-permute-start(bf16[256,256]{1,0:T(8,128)(2,1)S(1)} %constant_dynamic-update-slice_fusion.refs_0_), channel_id=1, source_target_pairs={{0,12},{1,13},{2,14},{3,15},{4,0},{5,1},{6,2},{7,3},{8,4},{9,5},{1... | collective-permute-start | bytes 393224 | tf_op jit(solution)/shard_map/ppermute | solution.py:279
  13.2 16.6 %collective-permute-start.4 = (bf16[256,256]{1,0:T(8,128)(2,1)S(1)}, bf16[256,256]{1,0:T(8,128)(2,1)S(1)}, u32[]{:S(2)}, u32[]{:S(2)}) collective-permute-start(bf16[256,256]{1,0:T(8,128)(2,1)S(1)} %constant_dynamic-update-slice_fusion.refs_0_), channel_id=1, source_target_pairs={{0,2},{1,3},{2,0},{3,1},{4,6},{5,7},{6,4},{7,5},{8,10},{9,11},{10,... | collective-permute-start | bytes 393224 | tf_op jit(solution)/shard_map/ppermute | solution.py:279
  14.4 15.4 %collective-permute-start.3 = (bf16[256,256]{1,0:T(8,128)(2,1)S(1)}, bf16[256,256]{1,0:T(8,128)(2,1)}, u32[]{:S(2)}, u32[]{:S(2)}) collective-permute-start(bf16[256,256]{1,0:T(8,128)(2,1)S(1)} %constant_dynamic-update-slice_fusion.refs_0_), channel_id=1, source_target_pairs={{0,8},{1,9},{2,10},{3,11},{4,12},{5,13},{6,14},{7,15},{8,0},{9,1},... | collective-permute-start | bytes 393224 | tf_op jit(solution)/shard_map/ppermute | solution.py:279
  15.0 16.0 %collective-permute-start.2 = (bf16[256,256]{1,0:T(8,128)(2,1)S(1)}, bf16[256,256]{1,0:T(8,128)(2,1)}, u32[]{:S(2)}, u32[]{:S(2)}) collective-permute-start(bf16[256,256]{1,0:T(8,128)(2,1)S(1)} %constant_dynamic-update-slice_fusion.refs_0_), channel_id=1, source_target_pairs={{0,4},{1,5},{2,6},{3,7},{4,8},{5,9},{6,10},{7,11},{8,12},{9,13},{1... | collective-permute-start | bytes 393224 | tf_op jit(solution)/shard_map/ppermute | solution.py:279
  27.1 5.1 %collective-permute-start.1 = (bf16[256,256]{1,0:T(8,128)(2,1)S(1)}, bf16[256,256]{1,0:T(8,128)(2,1)S(1)}, u32[]{:S(2)}, u32[]{:S(2)}) collective-permute-start(bf16[256,256]{1,0:T(8,128)(2,1)S(1)} %collective-permute-done.refs_3_), channel_id=1, source_target_pairs={{0,2},{1,3},{2,0},{3,1},{4,6},{5,7},{6,4},{7,5},{8,10},{9,11},{10,... | collective-permute-start | bytes 393224 | tf_op jit(solution)/shard_map/ppermute | solution.py:279
  28.2 8.9 %collective-permute-start.7 = (bf16[256,256]{1,0:T(8,128)(2,1)S(1)}, bf16[256,256]{1,0:T(8,128)(2,1)}, u32[]{:S(2)}, u32[]{:S(2)}) collective-permute-start(bf16[256,256]{1,0:T(8,128)(2,1)S(1)} %constant_dynamic-update-slice_fusion.refs_0_), channel_id=1, source_target_pairs={{0,1},{1,0},{2,3},{3,2},{4,5},{5,4},{6,7},{7,6},{8,9},{9,8},{10,11... | collective-permute-start | bytes 393224 | tf_op jit(solution)/shard_map/ppermute | solution.py:279
  29.8 7.5 %collective-permute-start.11 = (bf16[256,256]{1,0:T(8,128)(2,1)S(1)}, bf16[256,256]{1,0:T(8,128)(2,1)}, u32[]{:S(2)}, u32[]{:S(2)}) collective-permute-start(bf16[256,256]{1,0:T(8,128)(2,1)S(1)} %collective-permute-done.4.refs_4_), channel_id=1, source_target_pairs={{0,1},{1,0},{2,3},{3,2},{4,5},{5,4},{6,7},{7,6},{8,9},{9,8},{10,11... | collective-permute-start | bytes 393224 | tf_op jit(solution)/shard_map/ppermute | solution.py:279
  29.8 8.0 %collective-permute-start.6 = (bf16[256,256]{1,0:T(8,128)(2,1)}, bf16[256,256]{1,0:T(8,128)(2,1)}, u32[]{:S(2)}, u32[]{:S(2)}) collective-permute-start(bf16[256,256]{1,0:T(8,128)(2,1)} %collective-permute-done.3.refs_2_), channel_id=1, source_target_pairs={{0,2},{1,3},{2,0},{3,1},{4,6},{5,7},{6,4},{7,5},{8,10},{9,11},{10,... | collective-permute-start | bytes 393224 | tf_op jit(solution)/shard_map/ppermute | solution.py:279
  31.0 6.9 %collective-permute-start.5 = (bf16[256,256]{1,0:T(8,128)(2,1)}, bf16[256,256]{1,0:T(8,128)(2,1)}, u32[]{:S(2)}, u32[]{:S(2)}) collective-permute-start(bf16[256,256]{1,0:T(8,128)(2,1)} %collective-permute-done.2.refs_1_), channel_id=1, source_target_pairs={{0,2},{1,3},{2,0},{3,1},{4,6},{5,7},{6,4},{7,5},{8,10},{9,11},{10,... | collective-permute-start | bytes 393224 | tf_op jit(solution)/shard_map/ppermute | solution.py:279
  32.2 0.7 %copy-start.3 = (bf16[256,256]{1,0:T(8,128)(2,1)}, bf16[256,256]{1,0:T(8,128)(2,1)S(1)}, u32[]{:S(2)}) copy-start(bf16[256,256]{1,0:T(8,128)(2,1)S(1)} %collective-permute-done.1.refs_7_) | copy-start | bytes 393220
  32.8 6.2 %collective-permute-start.9 = (bf16[256,256]{1,0:T(8,128)(2,1)}, bf16[256,256]{1,0:T(8,128)(2,1)}, u32[]{:S(2)}, u32[]{:S(2)}) collective-permute-start(bf16[256,256]{1,0:T(8,128)(2,1)} %collective-permute-done.3.refs_2_), channel_id=1, source_target_pairs={{0,1},{1,0},{2,3},{3,2},{4,5},{5,4},{6,7},{7,6},{8,9},{9,8},{10,11... | collective-permute-start | bytes 393224 | tf_op jit(solution)/shard_map/ppermute | solution.py:279
  34.0 5.0 %copy-start.4 = (bf16[256,256]{1,0:T(8,128)(2,1)S(1)}, bf16[256,256]{1,0:T(8,128)(2,1)}, u32[]{:S(2)}) copy-start(bf16[256,256]{1,0:T(8,128)(2,1)} %copy-done.3) | copy-start | bytes 393220
  37.2 2.1 %collective-permute-start.8 = (bf16[256,256]{1,0:T(8,128)(2,1)}, bf16[256,256]{1,0:T(8,128)(2,1)S(1)}, u32[]{:S(2)}, u32[]{:S(2)}) collective-permute-start(bf16[256,256]{1,0:T(8,128)(2,1)} %collective-permute-done.2.refs_1_), channel_id=1, source_target_pairs={{0,1},{1,0},{2,3},{3,2},{4,5},{5,4},{6,7},{7,6},{8,9},{9,8},{10,11... | collective-permute-start | bytes 393224 | tf_op jit(solution)/shard_map/ppermute | solution.py:279
  37.3 2.0 %collective-permute-start.10 = (bf16[256,256]{1,0:T(8,128)(2,1)S(1)}, bf16[256,256]{1,0:T(8,128)(2,1)S(1)}, u32[]{:S(2)}, u32[]{:S(2)}) collective-permute-start(bf16[256,256]{1,0:T(8,128)(2,1)S(1)} %collective-permute-done.refs_3_), channel_id=1, source_target_pairs={{0,1},{1,0},{2,3},{3,2},{4,5},{5,4},{6,7},{7,6},{8,9},{9,8},{10,11... | collective-permute-start | bytes 393224 | tf_op jit(solution)/shard_map/ppermute | solution.py:279
  37.7 1.6 %collective-permute-start.13 = (bf16[256,256]{1,0:T(8,128)(2,1)}, bf16[256,256]{1,0:T(8,128)(2,1)S(1)}, u32[]{:S(2)}, u32[]{:S(2)}) collective-permute-start(bf16[256,256]{1,0:T(8,128)(2,1)} %collective-permute-done.6.refs_6_), channel_id=1, source_target_pairs={{0,1},{1,0},{2,3},{3,2},{4,5},{5,4},{6,7},{7,6},{8,9},{9,8},{10,11... | collective-permute-start | bytes 393224 | tf_op jit(solution)/shard_map/ppermute | solution.py:279
  37.9 2.3 %collective-permute-start.12 = (bf16[256,256]{1,0:T(8,128)(2,1)}, bf16[256,256]{1,0:T(8,128)(2,1)S(1)}, u32[]{:S(2)}, u32[]{:S(2)}) collective-permute-start(bf16[256,256]{1,0:T(8,128)(2,1)} %collective-permute-done.5.refs_5_), channel_id=1, source_target_pairs={{0,1},{1,0},{2,3},{3,2},{4,5},{5,4},{6,7},{7,6},{8,9},{9,8},{10,11... | collective-permute-start | bytes 393224 | tf_op jit(solution)/shard_map/ppermute | solution.py:279
  39.0 1.4 %collective-permute-start.14 = (bf16[256,256]{1,0:T(8,128)(2,1)S(1)}, bf16[256,256]{1,0:T(8,128)(2,1)S(1)}, u32[]{:S(2)}, u32[]{:S(2)}) collective-permute-start(bf16[256,256]{1,0:T(8,128)(2,1)S(1)} %copy-done.4), channel_id=1, source_target_pairs={{0,1},{1,0},{2,3},{3,2},{4,5},{5,4},{6,7},{7,6},{8,9},{9,8},{10,11... | collective-permute-start | bytes 393224 | tf_op jit(solution)/shard_map/ppermute | solution.py:279
